TPU v7x, 32 devices: a whole 2x2x4 slice. The times are simulated.
32 devices in a mesh: loop: 8 (over y, x, core), tp: 4 (over z).
Axes of the slice: x: 2, y: 2, z: 4, core: 2. Of those that a mesh axis runs over, the one named last changes fastest.
Arguments:
- tokens: bfloat16 [2048, 4096], P('loop', 'tp'), may hold values from -6 to 6
- out_grad: bfloat16 [2048, 6144], P('loop', 'tp'), may hold values from -6 to 6
- qkv_weight: bfloat16 [3, 4096, 6144], P(None, 'loop', 'tp'), may hold values from -0.09375 to 0.09375
- dest_row: int32 [2048], P('loop'), may hold values from 0 to 383, as said below
- loop_modality: int32 [8], replicated, may hold values from 0 to 2, as said below
Outputs:
- projected: bfloat16 [2048, 6144], P('loop', 'tp')
- input_grad: bfloat16 [2048, 4096], P('loop', 'tp')
- weight_grad: bfloat16 [3, 4096, 6144], P(None, 'loop', 'tp')
Inputs may be any that keep to these rules, and one draw needn't show every extreme that they name: `dest_row`: within each aligned block of 256 tokens the values are distinct, so at most 48 tokens of one block name one loop; in every draw some loop is named by exactly 48 tokens of every block. `loop_modality`: A quarter of the loops hold 0, half hold 1, a quarter hold 2.
All inputs are finite; a program needn't handle non-finite values.
Results may differ from a plain program's by a relative error of at most 0.014.
Values may be sent and summed in bfloat16 or wider, within the bound.
No kernel may reach another device: no remote copies, remote signals or barrier semaphores. Data moves between devices by JAX's collectives and lax.ppermute only.
A program may use at most 128 MiB of HBM per device.

v0:
```python
import functools
import math

import jax
import jax.numpy as jnp
from jax import lax
from jax.experimental import pallas as pl
from jax.experimental.pallas import tpu as pltpu
from jax.sharding import PartitionSpec as P


BF16 = jnp.bfloat16
F32 = jnp.float32
KIND_ROWS = 8
PROJECT_TILE = 512
WEIGHT_TILE = 512


def pack_kernel(kinds_of_loops, dest, grads, *outs, capacity):
    slots = dest[...]
    found = jnp.full(slots.shape, kinds_of_loops[0], jnp.int32)
    for loop_index in range(1, kinds_of_loops.shape[0]):
        found = jnp.where(slots >= loop_index * capacity, kinds_of_loops[loop_index], found)
    cut = slots.shape[1] // len(outs)
    for part, out in enumerate(outs):
        extra = out.shape[0] - cut
        kind = found[:, part * cut:(part + 1) * cut].astype(F32).astype(BF16)
        out[:cut] = grads[part * cut:(part + 1) * cut]
        out[cut:] = jnp.zeros((extra, out.shape[1]), BF16)
        out[cut:, :cut] = jnp.broadcast_to(kind, (extra, cut))


def packed_grads(out_grad, dest_row, loop_modality, capacity):
    rows, columns = out_grad.shape
    slots = dest_row.reshape(1, -1)
    packed = (rows // 2 + KIND_ROWS, columns)
    return pl.pallas_call(
        functools.partial(pack_kernel, capacity=capacity),
        grid_spec=pltpu.PrefetchScalarGridSpec(
            num_scalar_prefetch=1,
            grid=(1,),
            in_specs=[whole(slots.shape), whole(out_grad.shape)],
            out_specs=[whole(packed), whole(packed)],
        ),
        out_shape=[pltpu.HBM(packed, BF16)] * 2,
        compiler_params=limit(8),
    )(loop_modality, *in_hbm(slots, out_grad))


def in_hbm(*values):
    return [pltpu.with_memory_space_constraint(value, pltpu.HBM) for value in values]


def kinds_in(refs):
    return jnp.concatenate([ref[:1].astype(F32) for ref in refs], axis=1)


def kind_spec(half_block):
    cut = half_block.shape[0] - KIND_ROWS
    return pl.BlockSpec((KIND_ROWS, cut), lambda *_: (cut // KIND_ROWS, 0))


def pick(kind, products):
    chosen = products[0]
    for index in range(1, len(products)):
        chosen = jnp.where(kind == index, products[index], chosen)
    return chosen


def whole(shape):
    return pl.BlockSpec(shape, lambda *_: (0,) * len(shape))


def split_rows(value, outs):
    start = 0
    for out in outs:
        yield out, value[start:start + out.shape[0]]
        start += out.shape[0]


def limit(mebibytes):
    return pltpu.CompilerParams(vmem_limit_bytes=mebibytes << 20)


def input_kernel(core, own_weight, other_weight, *refs, blocks, tile):
    cut = refs[0].shape[0] - KIND_ROWS
    rhs = jnp.concatenate([ref[:cut] for ref in refs[:blocks]], axis=0)
    kind = kinds_in([ref[cut:, :cut] for ref in refs[:blocks]])
    outs = refs[blocks:]
    half = outs[0].shape[1] // 2
    kinds, _, columns = own_weight.shape
    for weight, side in ((own_weight, core[0]), (other_weight, 1 - core[0])):
        product = lax.dot_general(
            weight[...].reshape(kinds * tile, columns), rhs, (((1,), (1,)), ((), ())),
            preferred_element_type=F32,
        )
        products = [product[index * tile:(index + 1) * tile] for index in range(kinds)]
        chosen = pick(kind, products).astype(BF16).T
        at = pl.multiple_of(side * half + pl.program_id(0) * tile, tile)
        for out, part in split_rows(chosen, outs):
            out[:, pl.ds(at, tile)] = part


def input_terms(core, blocks, sizes, own_weight, other_weight):
    kinds, half, columns = own_weight.shape
    tile = min(half, 256)
    weight_spec = pl.BlockSpec((kinds, tile, columns), lambda step, core: (0, step, 0))
    return pl.pallas_call(
        functools.partial(input_kernel, blocks=len(blocks), tile=tile),
        grid_spec=pltpu.PrefetchScalarGridSpec(
            num_scalar_prefetch=1,
            grid=(half // tile,),
            in_specs=[weight_spec, weight_spec] + [whole(block.shape) for block in blocks],
            out_specs=[whole((size, 2 * half)) for size in sizes],
        ),
        out_shape=[pltpu.HBM((size, 2 * half), BF16) for size in sizes],
        compiler_params=limit(28),
    )(core, *in_hbm(own_weight, other_weight, *blocks))


def project_kernel(core, own_weight, other_weight, *refs, items):
    _, half, tile = own_weight.shape
    own_at = pl.multiple_of(core[0] * half, half)
    other_at = pl.multiple_of((1 - core[0]) * half, half)
    own = jnp.concatenate([ref[:, pl.ds(own_at, half)] for ref in refs[:items]], axis=0)
    other = jnp.concatenate([ref[:, pl.ds(other_at, half)] for ref in refs[:items]], axis=0)
    kind = kinds_in([ref[...] for ref in refs[items:2 * items]])
    row_kind = jnp.broadcast_to(kind, (tile, kind.shape[1])).T
    products = [
        jnp.dot(own, own_weight[index], preferred_element_type=F32)
        + jnp.dot(other, other_weight[index], preferred_element_type=F32)
        for index in range(own_weight.shape[0])
    ]
    chosen = pick(row_kind, products).astype(BF16)
    for out, part in split_rows(chosen, refs[2 * items:]):
        out[...] = part


def project_parts(core, items, own_weight, other_weight):
    kinds, half, columns = own_weight.shape
    tile = math.gcd(columns, PROJECT_TILE)
    weight_spec = pl.BlockSpec((kinds, half, tile), lambda step, core: (0, 0, step))
    cut = items[0][2].shape[0] - KIND_ROWS
    return pl.pallas_call(
        functools.partial(project_kernel, items=len(items)),
        grid_spec=pltpu.PrefetchScalarGridSpec(
            num_scalar_prefetch=1,
            grid=(columns // tile,),
            in_specs=[weight_spec, weight_spec]
            + [pl.BlockSpec((cut, 2 * half), lambda step, core, part=item[1]: (part, 0)) for item in items]
            + [kind_spec(item[2]) for item in items],
            out_specs=[pl.BlockSpec((cut, tile), lambda step, core: (0, step))] * len(items),
        ),
        out_shape=[pltpu.HBM((cut, columns), BF16)] * len(items),
        compiler_params=limit(28),
    )(core, *in_hbm(own_weight, other_weight, *[item[0] for item in items], *[item[2] for item in items]))


def total_kernel(*refs, counts):
    outs = refs[sum(counts):]
    start = 0
    for count, out in zip(counts, outs):
        total = refs[start][...].astype(F32)
        for ref in refs[start + 1:start + count]:
            total = total + ref[...].astype(F32)
        out[...] = total.astype(BF16)
        start += count


def totals(groups):
    values = [value for group in groups for value in group]
    return pl.pallas_call(
        functools.partial(total_kernel, counts=[len(group) for group in groups]),
        grid=(1,),
        in_specs=[whole(value.shape) for value in values],
        out_specs=[whole(group[0].shape) for group in groups],
        out_shape=[pltpu.HBM(group[0].shape, BF16) for group in groups],
        compiler_params=limit(16),
    )(*in_hbm(*values))


def finish_kernel(*refs, count):
    out = refs[-1]
    cut = out.shape[0] // 2
    for part in (0, 1):
        total = refs[part * count][...].astype(F32)
        for ref in refs[part * count + 1:(part + 1) * count]:
            total = total + ref[...].astype(F32)
        out[part * cut:(part + 1) * cut] = total.astype(BF16)


def finish(first, second):
    cut, columns = first[0].shape
    return pl.pallas_call(
        functools.partial(finish_kernel, count=len(first)),
        grid=(1,),
        in_specs=[whole((cut, columns))] * (2 * len(first)),
        out_specs=whole((2 * cut, columns)),
        out_shape=jax.ShapeDtypeStruct((2 * cut, columns), BF16),
        compiler_params=limit(16),
    )(*in_hbm(*first, *second))


def fold_kernel(wanted, *refs, sources, counts):
    places = len(counts)
    added = refs[sources:sources + sum(counts)]
    outs = refs[sources + sum(counts):-2]
    held, done = refs[-2:]
    for place in range(places):
        for index in range(sources):
            @pl.when(wanted[place] == index)
            def _(place=place, index=index):
                pltpu.make_async_copy(refs[index], held.at[place], done.at[place]).start()
    start = 0
    for place, (count, out) in enumerate(zip(counts, outs)):
        pltpu.make_async_copy(refs[0], held.at[place], done.at[place]).wait()
        if count:
            total = held[place].astype(F32)
            for ref in added[start:start + count]:
                total = total + ref[...].astype(F32)
            out[...] = total.astype(BF16)
        else:
            out[...] = held[place]
        start += count


def fold(wanted, sources, groups):
    shape = sources[0].shape
    values = [value for group in groups for value in group]
    return pl.pallas_call(
        functools.partial(fold_kernel, sources=len(sources), counts=[len(group) for group in groups]),
        grid_spec=pltpu.PrefetchScalarGridSpec(
            num_scalar_prefetch=1,
            grid=(1,),
            in_specs=[pl.BlockSpec(memory_space=pl.ANY)] * len(sources) + [whole(shape)] * len(values),
            out_specs=[whole(shape)] * len(groups),
            scratch_shapes=[
                pltpu.VMEM((len(groups), *shape), BF16), pltpu.SemaphoreType.DMA((len(groups),))
            ],
        ),
        out_shape=[pltpu.HBM(shape, BF16)] * len(groups),
        compiler_params=limit(20),
    )(jnp.stack(wanted), *sources, *values)


def weight_kernel(core, *refs, blocks, grads, scale):
    rows = refs[:blocks]
    columns_of = refs[blocks:blocks + grads]
    kind_rows = refs[blocks + grads:blocks + 2 * grads]
    out, turned = refs[blocks + 2 * grads:]
    kinds, _, _ = out.shape

    @pl.when(pl.program_id(0) == 0)
    def _():
        kind = kinds_in([ref[...] for ref in kind_rows])
        start = 0
        for ref in rows:
            count = ref.shape[0]
            part = ref[...].T
            own_kind = kind[:, start:start + count]
            for which in range(kinds):
                turned[which, :, start:start + count] = jnp.where(own_kind == which, part, 0)
            start += count

    columns = jnp.concatenate([ref[...] for ref in columns_of], axis=0)
    for which in range(kinds):
        total = jnp.dot(turned[which], columns, preferred_element_type=F32)
        out[which] = (total * scale).astype(BF16)


def weight_gradient(core, blocks, half_blocks, kinds, scale):
    rows, features = blocks[0].shape
    half = features // 2
    columns = half_blocks[0].shape[1]
    cut = half_blocks[0].shape[0] - KIND_ROWS
    tile = math.gcd(columns, WEIGHT_TILE)
    return pl.pallas_call(
        functools.partial(weight_kernel, blocks=len(blocks), grads=len(half_blocks), scale=scale),
        grid_spec=pltpu.PrefetchScalarGridSpec(
            num_scalar_prefetch=1,
            grid=(columns // tile,),
            in_specs=[pl.BlockSpec((rows, half), lambda step, core: (0, core[0])) for _ in blocks]
            + [pl.BlockSpec((cut, tile), lambda step, core: (0, step)) for _ in half_blocks]
            + [kind_spec(block) for block in half_blocks],
            out_specs=pl.BlockSpec((kinds, half, tile), lambda step, core: (0, 0, step)),
            scratch_shapes=[pltpu.VMEM((kinds, half, rows * len(blocks)), BF16)],
        ),
        out_shape=jax.ShapeDtypeStruct((kinds, half, columns), BF16),
        compiler_params=limit(36),
    )(core, *in_hbm(*blocks, *half_blocks, *half_blocks))


def low_high(offset):
    return offset & -offset, 1 << (offset.bit_length() - 1)


def body(tokens, out_grad, qkv_weight, dest_row, loop_modality):
    loop_count = lax.axis_size("loop")
    tp_count = lax.axis_size("tp")
    row_count, feature_part = tokens.shape
    kinds, half, _ = qkv_weight.shape
    chip_count = loop_count // 2
    assert chip_count == tp_count and 2 * half == feature_part
    capacity = 3 * row_count // (2 * loop_count)
    grad_scale = 1.0 / math.sqrt(row_count * loop_count)
    loop_index = lax.axis_index("loop")
    chip, level = loop_index >> 1, lax.axis_index("tp")
    core = (loop_index & 1).reshape(1)
    bits = [1 << place for place in range(chip_count.bit_length() - 1)]
    offsets = sorted(range(1, chip_count), key=lambda offset: (bin(offset).count("1"), offset))
    several = [offset for offset in offsets if offset & (offset - 1)]

    def across(value, offset):
        pairs = [(i, i ^ (2 * offset)) for i in range(loop_count)]
        return lax.ppermute(value, "loop", pairs)

    def sibling(value):
        return lax.ppermute(value, "loop", [(i, i ^ 1) for i in range(loop_count)])

    def line_pairs(parity, stage):
        pairs = []
        for low in range(parity, tp_count - 1, 2):
            if low - stage + 1 >= 0:
                pairs.append((low, low + 1))
            if low + stage <= tp_count - 1:
                pairs.append((low + 1, low))
        return pairs

    def along(value, pairs):
        return lax.ppermute(value, "tp", pairs)

    stages = range(1, tp_count)
    facing = [jnp.where(level % 2 == parity, 1, -1) for parity in (0, 1)]

    other_weight = sibling(qkv_weight)
    came = {(0, 0): tokens, (1, 0): tokens}
    for stage in stages:
        for parity in (0, 1):
            pairs = line_pairs(parity, stage)
            if pairs:
                came[parity, stage] = along(came[1 - parity, stage - 1], pairs)

    own_grad = packed_grads(out_grad, dest_row, loop_modality, capacity)
    grads = {0: own_grad}
    for bit in bits:
        grads[bit] = [None, None]
    for bit in bits:
        first = 0 if bit == bits[-1] else 1
        for part in (first, 1 - first):
            grads[bit][part] = across(own_grad[part], bit)
    for offset in several:
        low, high = low_high(offset)
        grads[offset] = [across(grads[offset ^ low][0], low), across(grads[offset ^ high][1], high)]

    def halves_of(group):
        return [part for offset in group for part in grads[offset]]

    arrived = {}
    for group in ([0], bits, several):
        made = input_terms(core, halves_of(group), [row_count] * len(group), qkv_weight, other_weight)
        for offset, term in zip(group, made):
            arrived[offset] = across(term, offset) if offset else term
    all_terms = [arrived[offset] for offset in range(chip_count)]

    def term_number(where):
        return chip ^ jnp.clip(where, 0, tp_count - 1)

    back = {}
    for stage in reversed(stages):
        links = [parity for parity in (0, 1) if line_pairs(parity, stage)]
        wanted = [term_number(level + stage * facing[parity]) for parity in links]
        groups = [[back[1 - parity, stage + 1]] if (1 - parity, stage + 1) in back else [] for parity in links]
        made = fold(wanted, all_terms, groups)
        for parity, value in zip(links, made):
            pairs = [(b, a) for a, b in line_pairs(parity, stage)]
            back[parity, stage] = along(value, pairs)
    last = [back[parity, 1] for parity in (0, 1) if (parity, 1) in back]
    input_grad = fold([term_number(level)], all_terms, [last])[0]

    places = [place for place in came if place != (1, 0)]
    sources = [came[place] for place in places]
    wanted = []
    for offset in range(chip_count):
        where = chip ^ offset
        index = jnp.int32(0)
        for number, (parity, stage) in enumerate(places):
            if stage:
                index = jnp.where(where == level + stage * facing[parity], number, index)
        wanted.append(index)
    sends = fold(wanted, in_hbm(*sources), [[]] * chip_count)
    rows = {offset: across(sends[offset], offset) if offset else sends[offset] for offset in range(chip_count)}

    pieces = {(offset, part): [] for offset in range(chip_count) for part in (0, 1)}

    def project(places):
        items = [(rows[offset], part, grads[offset][part]) for offset, part in places]
        made = project_parts(core, items, qkv_weight, other_weight)
        return dict(zip(places, made))

    own_parts = project([(0, 0), (0, 1)])
    for weight in range(len(bits), 0, -1):
        places = [(offset, part) for offset in offsets if bin(offset).count("1") == weight for part in (0, 1)]
        made = project(places)
        summed = [place for place in places if pieces[place]]
        if summed:
            sums = totals([[made[place], *pieces[place]] for place in summed])
            made.update(zip(summed, sums))
        for offset, part in places:
            link = offset if offset in bits else low_high(offset)[part]
            piece = across(made[offset, part], link)
            pieces[offset ^ link, part].append(piece)
    projected = finish([own_parts[0, 0], *pieces[0, 0]], [own_parts[0, 1], *pieces[0, 1]])

    near = [rows[offset] for offset in range(chip_count)]
    far = [sibling(block) for block in near]
    near_grads = halves_of(range(chip_count))
    far_grads = [sibling(block) for block in near_grads]
    weight_grad = weight_gradient(core, near + far, near_grads + far_grads, kinds, grad_scale)
    return projected, input_grad, weight_grad


def solution(mesh):
    placed = (P("loop", "tp"), P("loop", "tp"), P(None, "loop", "tp"), P("loop"), P())
    return jax.shard_map(
        body,
        mesh=mesh,
        in_specs=placed,
        out_specs=(P("loop", "tp"), P("loop", "tp"), P(None, "loop", "tp")),
        check_vma=False,
    )
```

profile of v0, /device:TPU:0, one launch (start us, length us, event | category | flops | bytes accessed | tf_op | source)
XLA Modules:
  0.0 174.2 jit_solution(9931932090435020649)
XLA Ops:
  1.8 2.6 %shard_map.77 = (bf16[136,1536]{1,0:T(8,128)(2,1)}, bf16[136,1536]{1,0:T(8,128)(2,1)}) custom-call(s32[8]{0:T(128)S(1)} %copy-done.2, s32[1,256]{1,0:T(1,128)} %bitcast.12, bf16[256,1536]{1,0:T(8,128)(2,1)} %grads.1), custom_call_target="tpu_custom_call" | custom-call | tf_op jit(solution)/shard_map/pallas_call | solution.py:37
  4.5 3.0 %collective-permute-start.10 = (bf16[136,1536]{1,0:T(8,128)(2,1)}, bf16[136,1536]{1,0:T(8,128)(2,1)S(1)}, u32[]{:S(2)}, u32[]{:S(2)}) collective-permute-start(bf16[136,1536]{1,0:T(8,128)(2,1)} %get-tuple-element.26.refs_2_.refs_0_.refs_8_.refs_24_), channel_id=1, source_target_pairs={{0,16},{4,20},{8,24},{12,28},{16,0},{20,4},{24,8},{28,12},{1,17},{... | collective-permute-start | bytes 1253384 | tf_op jit(solution)/shard_map/ppermute | solution.py:315
  7.5 1.5 collective-permute-start.8
  9.5 2.9 %collective-permute-start.11 = (bf16[136,1536]{1,0:T(8,128)(2,1)}, bf16[136,1536]{1,0:T(8,128)(2,1)S(1)}, u32[]{:S(2)}, u32[]{:S(2)}) collective-permute-start(bf16[136,1536]{1,0:T(8,128)(2,1)} %get-tuple-element.27.refs_3_.refs_1_.refs_9_.refs_25_), channel_id=1, source_target_pairs={{0,16},{4,20},{8,24},{12,28},{16,0},{20,4},{24,8},{28,12},{1,17},{... | collective-permute-start | bytes 1253384 | tf_op jit(solution)/shard_map/ppermute | solution.py:315
  12.4 5.8 %collective-permute-done.10.refs_6_.refs_2_.refs_12_.refs_28_ = bf16[136,1536]{1,0:T(8,128)(2,1)S(1)} collective-permute-done((bf16[136,1536]{1,0:T(8,128)(2,1)}, bf16[136,1536]{1,0:T(8,128)(2,1)S(1)}, u32[]{:S(2)}, u32[]{:S(2)}) %collective-permute-start.10) | collective-permute-done | bytes 417824 | tf_op jit(solution)/shard_map/ppermute | solution.py:315
  18.2 2.1 %collective-permute-start.1 = (bf16[256,1024]{1,0:T(8,128)(2,1)}, bf16[256,1024]{1,0:T(8,128)(2,1)}, u32[]{:S(2)}, u32[]{:S(2)}) collective-permute-start(bf16[256,1024]{1,0:T(8,128)(2,1)} %refs_0_.1), channel_id=1, source_target_pairs={{0,1},{1,0},{2,3},{3,2},{4,5},{5,4},{6,7},{7,6},{8,9},{9,8},{10,11... | collective-permute-start | bytes 1572872 | tf_op jit(solution)/shard_map/ppermute | solution.py:330
  20.3 1.5 collective-permute-start.9
  22.3 4.2 %collective-permute-done.11.refs_7_.refs_3_.refs_13_.refs_29_ = bf16[136,1536]{1,0:T(8,128)(2,1)S(1)} collective-permute-done((bf16[136,1536]{1,0:T(8,128)(2,1)}, bf16[136,1536]{1,0:T(8,128)(2,1)S(1)}, u32[]{:S(2)}, u32[]{:S(2)}) %collective-permute-start.11) | collective-permute-done | bytes 417824 | tf_op jit(solution)/shard_map/ppermute | solution.py:315
  28.0 5.2 %collective-permute-done.9.refs_5_.refs_1_.refs_11_.refs_27_ = bf16[136,1536]{1,0:T(8,128)(2,1)} collective-permute-done((bf16[136,1536]{1,0:T(8,128)(2,1)}, bf16[136,1536]{1,0:T(8,128)(2,1)}, u32[]{:S(2)}, u32[]{:S(2)}) %collective-permute-start.9) | collective-permute-done | bytes 417824 | tf_op jit(solution)/shard_map/ppermute | solution.py:315
  33.1 1.5 collective-permute-start.15
  36.2 9.2 %shard_map.84 = (bf16[256,1024]{1,0:T(8,128)(2,1)}, bf16[256,1024]{1,0:T(8,128)(2,1)}) custom-call(s32[1]{0:T(128)} %bitcast.core, bf16[3,512,1536]{2,1,0:T(8,128)(2,1)} %own_weight.11, bf16[3,512,1536]{2,1,0:T(8,128)(2,1)} %collective-permute-done.other_weight, bf16[136,1536]{1,0:T(8,128)(2,1)} %copy-done.4, ...), custom_call_target="tpu_custom_call" | custom-call | tf_op jit(solution)/shard_map/pallas_call | solution.py:108
  45.4 1.6 collective-permute-start.21
  47.5 6.4 %shard_map.85 = bf16[256,1024]{1,0:T(8,128)(2,1)} custom-call(s32[1]{0:T(128)} %bitcast.core, bf16[3,512,1536]{2,1,0:T(8,128)(2,1)} %own_weight.11, bf16[3,512,1536]{2,1,0:T(8,128)(2,1)} %collective-permute-done.other_weight, bf16[136,1536]{1,0:T(8,128)(2,1)} %collective-permute-done.14.refs_2_.refs_0_.refs_14_.refs_30_, ...), custom_call_target="tpu_custom_call" | custom-call | tf_op jit(solution)/shard_map/pallas_call | solution.py:108
  58.0 2.5 %collective-permute-done.21.refs_1_ = bf16[256,1024]{1,0:T(8,128)(2,1)S(1)} collective-permute-done((bf16[256,1024]{1,0:T(8,128)(2,1)}, bf16[256,1024]{1,0:T(8,128)(2,1)S(1)}, u32[]{:S(2)}, u32[]{:S(2)}) %collective-permute-start.21) | collective-permute-done | bytes 524320 | tf_op jit(solution)/shard_map/ppermute | solution.py:315
  60.5 12.0 %collective-permute-done.22.refs_2_ = bf16[256,1024]{1,0:T(8,128)(2,1)S(1)} collective-permute-done((bf16[256,1024]{1,0:T(8,128)(2,1)}, bf16[256,1024]{1,0:T(8,128)(2,1)S(1)}, u32[]{:S(2)}, u32[]{:S(2)}) %collective-permute-start.22) | collective-permute-done | bytes 524320 | tf_op jit(solution)/shard_map/ppermute | solution.py:315
  73.0 6.3 %shard_map.83.refs_0_ = bf16[256,1024]{1,0:T(8,128)(2,1)} custom-call(s32[1]{0:T(128)} %bitcast.core, bf16[3,512,1536]{2,1,0:T(8,128)(2,1)} %own_weight.11, bf16[3,512,1536]{2,1,0:T(8,128)(2,1)} %collective-permute-done.other_weight, bf16[136,1536]{1,0:T(8,128)(2,1)} %get-tuple-element.26.refs_2_.refs_0_.refs_8_.refs_24_, ...), custom_call_target="tpu_custom_call" | custom-call | tf_op jit(solution)/shard_map/pallas_call | solution.py:108
  81.4 2.2 %collective-permute-done.5.refs_5_ = bf16[256,1024]{1,0:T(8,128)(2,1)} collective-permute-done((bf16[256,1024]{1,0:T(8,128)(2,1)}, bf16[256,1024]{1,0:T(8,128)(2,1)}, u32[]{:S(2)}, u32[]{:S(2)}) %collective-permute-start.5) | collective-permute-done | bytes 524320 | tf_op jit(solution)/shard_map/ppermute | solution.py:330
  83.6 3.4 %collective-permute-start.24 = (bf16[256,1024]{1,0:T(8,128)(2,1)}, bf16[256,1024]{1,0:T(8,128)(2,1)S(1)}, u32[]{:S(2)}, u32[]{:S(2)}) collective-permute-start(bf16[256,1024]{1,0:T(8,128)(2,1)} %shard_map.86), channel_id=1, source_target_pairs={{0,1},{3,2},{4,5},{7,6},{8,9},{11,10},{12,13},{15,14},{16,17},{19,... | collective-permute-start | bytes 1572872 | tf_op jit(solution)/shard_map/ppermute | solution.py:330
  87.1 3.4 %shard_map.76 = (bf16[256,1024]{1,0:T(8,128)(2,1)}, bf16[256,1024]{1,0:T(8,128)(2,1)}, bf16[256,1024]{1,0:T(8,128)(2,1)}, bf16[256,1024]{1,0:T(8,128)(2,1)}) custom-call(s32[4]{0:T(128)S(1)} %pad_add_fusion.wanted, bf16[256,1024]{1,0:T(8,128)(2,1)} %refs_0_.1, bf16[256,1024]{1,0:T(8,128)(2,1)} %collective-permute-done.1.refs_1_, ...), custom_call_target="tpu_custom_call" | custom-call | tf_op jit(solution)/shard_map/pallas_call | solution.py:230
  92.3 1.8 %collective-permute-start.13 = (bf16[256,1024]{1,0:T(8,128)(2,1)}, bf16[256,1024]{1,0:T(8,128)(2,1)}, u32[]{:S(2)}, u32[]{:S(2)}) collective-permute-start(bf16[256,1024]{1,0:T(8,128)(2,1)} %get-tuple-element.33), channel_id=1, source_target_pairs={{0,24},{4,28},{8,16},{12,20},{16,8},{20,12},{24,0},{28,4},{1,25},{... | collective-permute-start | bytes 1572872 | tf_op jit(solution)/shard_map/ppermute | solution.py:315
  94.2 4.9 %collective-permute-done.24.refs_4_ = bf16[256,1024]{1,0:T(8,128)(2,1)S(1)} collective-permute-done((bf16[256,1024]{1,0:T(8,128)(2,1)}, bf16[256,1024]{1,0:T(8,128)(2,1)S(1)}, u32[]{:S(2)}, u32[]{:S(2)}) %collective-permute-start.24) | collective-permute-done | bytes 524320 | tf_op jit(solution)/shard_map/ppermute | solution.py:330
  99.2 1.7 shard_map.87
  100.9 4.8 %collective-permute-done.6.refs_0_.refs_1_ = bf16[256,1024]{1,0:T(8,128)(2,1)} collective-permute-done((bf16[256,1024]{1,0:T(8,128)(2,1)}, bf16[256,1024]{1,0:T(8,128)(2,1)}, u32[]{:S(2)}, u32[]{:S(2)}) %collective-permute-start.6) | collective-permute-done | bytes 524320 | tf_op jit(solution)/shard_map/ppermute | solution.py:315
  106.4 10.6 %collective-permute-done.7.refs_2_.refs_3_ = bf16[256,1024]{1,0:T(8,128)(2,1)} collective-permute-done((bf16[256,1024]{1,0:T(8,128)(2,1)}, bf16[256,1024]{1,0:T(8,128)(2,1)}, u32[]{:S(2)}, u32[]{:S(2)}) %collective-permute-start.7) | collective-permute-done | bytes 524320 | tf_op jit(solution)/shard_map/ppermute | solution.py:315
  119.0 6.7 %shard_map.80 = (bf16[128,1536]{1,0:T(8,128)(2,1)}, bf16[128,1536]{1,0:T(8,128)(2,1)}) custom-call(s32[1]{0:T(128)} %bitcast.core, bf16[3,512,1536]{2,1,0:T(8,128)(2,1)} %own_weight.11, bf16[3,512,1536]{2,1,0:T(8,128)(2,1)} %collective-permute-done.other_weight, bf16[256,1024]{1,0:T(8,128)(2,1)} %collective-permute-done.13.refs_0_.refs_1_.refs_3_, ...), custom_call_target="tpu_custom_call" | custom-call | tf_op jit(solution)/shard_map/pallas_call | solution.py:144
  127.8 8.5 %shard_map.79 = (bf16[128,1536]{1,0:T(8,128)(2,1)}, bf16[128,1536]{1,0:T(8,128)(2,1)}, bf16[128,1536]{1,0:T(8,128)(2,1)}, bf16[128,1536]{1,0:T(8,128)(2,1)}) custom-call(s32[1]{0:T(128)} %bitcast.core, bf16[3,512,1536]{2,1,0:T(8,128)(2,1)} %own_weight.11, bf16[3,512,1536]{2,1,0:T(8,128)(2,1)} %collective-permute-done.other_weight, ...), custom_call_target="tpu_custom_call" | custom-call | tf_op jit(solution)/shard_map/pallas_call | solution.py:144
  137.5 1.8 %shard_map.88 = (bf16[256,1024]{1,0:T(8,128)(2,1)}, bf16[256,1024]{1,0:T(8,128)(2,1)}) custom-call(s32[2]{0:T(128)S(1)} %pad_add_fusion.1.wanted, bf16[256,1024]{1,0:T(8,128)(2,1)S(1)} %copy-done.1, bf16[256,1024]{1,0:T(8,128)(2,1)S(1)} %collective-permute-done.21.refs_1_, bf16[256,1024]{1,0:T(8,128)(2,1)S(1)} %collective-permute-done.22.refs_2_, ...), custom_call_target="tpu_custom_call" | custom-call | tf_op jit(solution)/shard_map/pallas_call | solution.py:230
  140.3 2.3 %shard_map.81 = (bf16[128,1536]{1,0:T(8,128)(2,1)}, bf16[128,1536]{1,0:T(8,128)(2,1)}) custom-call(bf16[128,1536]{1,0:T(8,128)(2,1)} %get-tuple-element.32.refs_0_, bf16[128,1536]{1,0:T(8,128)(2,1)} %collective-permute-done.16.refs_1_, bf16[128,1536]{1,0:T(8,128)(2,1)} %get-tuple-element.35.refs_2_, bf16[128,1536]{1,0:T(8,128)(2,1)} %collective-permute-done.17.refs_3_), custom_call_target="tpu_custom_call" | custom-call | tf_op jit(solution)/shard_map/pallas_call | solution.py:172
  144.7 2.4 %collective-permute-done.12.refs_1_ = bf16[128,1536]{1,0:T(8,128)(2,1)S(1)} collective-permute-done((bf16[128,1536]{1,0:T(8,128)(2,1)}, bf16[128,1536]{1,0:T(8,128)(2,1)S(1)}, u32[]{:S(2)}, u32[]{:S(2)}) %collective-permute-start.12) | collective-permute-done | bytes 393248 | tf_op jit(solution)/shard_map/ppermute | solution.py:315
  148.2 15.1 %shard_map.90 = bf16[3,512,1536]{2,1,0:T(8,128)(2,1)} custom-call(s32[1]{0:T(128)} %bitcast.core, bf16[256,1024]{1,0:T(8,128)(2,1)} %get-tuple-element.25.refs_0_.refs_1_, bf16[256,1024]{1,0:T(8,128)(2,1)} %collective-permute-done.6.refs_0_.refs_1_, bf16[256,1024]{1,0:T(8,128)(2,1)} %collective-permute-done.7.refs_2_.refs_3_, ...), custom_call_target="tpu_custom_call" | custom-call | tf_op jit(solution)/shard_map/pallas_call | solution.py:277
  163.4 6.8 %shard_map.78 = (bf16[128,1536]{1,0:T(8,128)(2,1)}, bf16[128,1536]{1,0:T(8,128)(2,1)}) custom-call(s32[1]{0:T(128)} %bitcast.core, bf16[3,512,1536]{2,1,0:T(8,128)(2,1)} %own_weight.11, bf16[3,512,1536]{2,1,0:T(8,128)(2,1)} %collective-permute-done.other_weight, bf16[256,1024]{1,0:T(8,128)(2,1)} %get-tuple-element.25.refs_0_.refs_1_, ...), custom_call_target="tpu_custom_call" | custom-call | tf_op jit(solution)/shard_map/pallas_call | solution.py:144
  170.2 2.8 %shard_map.82 = bf16[256,1536]{1,0:T(8,128)(2,1)} custom-call(bf16[128,1536]{1,0:T(8,128)(2,1)} %get-tuple-element.28.refs_0_, bf16[128,1536]{1,0:T(8,128)(2,1)} %copy-done.13, bf16[128,1536]{1,0:T(8,128)(2,1)} %collective-permute-done.18.refs_2_, bf16[128,1536]{1,0:T(8,128)(2,1)} %get-tuple-element.38.refs_3_, ...), custom_call_target="tpu_custom_call" | custom-call | tf_op jit(solution)/shard_map/pallas_call | solution.py:194
  (96 shorter events, 25.5 us)
Async XLA Ops:
  0.6 35.5 %collective-permute-start = (bf16[3,512,1536]{2,1,0:T(8,128)(2,1)}, bf16[3,512,1536]{2,1,0:T(8,128)(2,1)}, u32[]{:S(2)}, u32[]{:S(2)}) collective-permute-start(bf16[3,512,1536]{2,1,0:T(8,128)(2,1)} %own_weight.11), channel_id=1, source_target_pairs={{0,4},{4,0},{8,12},{12,8},{16,20},{20,16},{24,28},{28,24},{1,5},{5... | collective-permute-start | bytes 14155784 | tf_op jit(solution)/shard_map/ppermute | solution.py:318
  9.5 17.0 %collective-permute-start.11 = (bf16[136,1536]{1,0:T(8,128)(2,1)}, bf16[136,1536]{1,0:T(8,128)(2,1)S(1)}, u32[]{:S(2)}, u32[]{:S(2)}) collective-permute-start(bf16[136,1536]{1,0:T(8,128)(2,1)} %get-tuple-element.27.refs_3_.refs_1_.refs_9_.refs_25_), channel_id=1, source_target_pairs={{0,16},{4,20},{8,24},{12,28},{16,0},{20,4},{24,8},{28,12},{1,17},{... | collective-permute-start | bytes 1253384 | tf_op jit(solution)/shard_map/ppermute | solution.py:315
  18.2 16.4 %collective-permute-start.1 = (bf16[256,1024]{1,0:T(8,128)(2,1)}, bf16[256,1024]{1,0:T(8,128)(2,1)}, u32[]{:S(2)}, u32[]{:S(2)}) collective-permute-start(bf16[256,1024]{1,0:T(8,128)(2,1)} %refs_0_.1), channel_id=1, source_target_pairs={{0,1},{1,0},{2,3},{3,2},{4,5},{5,4},{6,7},{7,6},{8,9},{9,8},{10,11... | collective-permute-start | bytes 1572872 | tf_op jit(solution)/shard_map/ppermute | solution.py:330
  21.8 23.6 %collective-permute-start.14 = (bf16[136,1536]{1,0:T(8,128)(2,1)S(1)}, bf16[136,1536]{1,0:T(8,128)(2,1)}, u32[]{:S(2)}, u32[]{:S(2)}) collective-permute-start(bf16[136,1536]{1,0:T(8,128)(2,1)S(1)} %collective-permute-done.10.refs_6_.refs_2_.refs_12_.refs_28_), channel_id=1, source_target_pairs={{0,8},{4,12},{8,0},{12,4},{16,24},{20,28},{24,16},{28,20},{1,9},{5... | collective-permute-start | bytes 1253384 | tf_op jit(solution)/shard_map/ppermute | solution.py:315
  26.5 27.4 %collective-permute-start.2 = (bf16[256,1024]{1,0:T(8,128)(2,1)}, bf16[256,1024]{1,0:T(8,128)(2,1)}, u32[]{:S(2)}, u32[]{:S(2)}) collective-permute-start(bf16[256,1024]{1,0:T(8,128)(2,1)} %refs_0_.1), channel_id=1, source_target_pairs={{1,2},{2,1},{5,6},{6,5},{9,10},{10,9},{13,14},{14,13},{17,18},{18,... | collective-permute-start | bytes 1572872 | tf_op jit(solution)/shard_map/ppermute | solution.py:330
  33.1 13.9 %collective-permute-start.15 = (bf16[136,1536]{1,0:T(8,128)(2,1)}, bf16[136,1536]{1,0:T(8,128)(2,1)}, u32[]{:S(2)}, u32[]{:S(2)}) collective-permute-start(bf16[136,1536]{1,0:T(8,128)(2,1)} %collective-permute-done.9.refs_5_.refs_1_.refs_11_.refs_27_), channel_id=1, source_target_pairs={{0,16},{4,20},{8,24},{12,28},{16,0},{20,4},{24,8},{28,12},{1,17},{... | collective-permute-start | bytes 1253384 | tf_op jit(solution)/shard_map/ppermute | solution.py:315
  34.6 22.0 %collective-permute-start.4 = (bf16[256,1024]{1,0:T(8,128)(2,1)}, bf16[256,1024]{1,0:T(8,128)(2,1)}, u32[]{:S(2)}, u32[]{:S(2)}) collective-permute-start(bf16[256,1024]{1,0:T(8,128)(2,1)} %collective-permute-done.1.refs_1_), channel_id=1, source_target_pairs={{1,2},{2,1},{5,6},{6,5},{9,10},{10,9},{13,14},{14,13},{17,18},{18,... | collective-permute-start | bytes 1572872 | tf_op jit(solution)/shard_map/ppermute | solution.py:330
  36.1 19.2 %collective-permute-start.37 = (bf16[136,1536]{1,0:T(8,128)(2,1)S(1)}, bf16[136,1536]{1,0:T(8,128)(2,1)S(1)}, u32[]{:S(2)}, u32[]{:S(2)}) collective-permute-start(bf16[136,1536]{1,0:T(8,128)(2,1)S(1)} %collective-permute-done.10.refs_6_.refs_2_.refs_12_.refs_28_), channel_id=1, source_target_pairs={{0,4},{4,0},{8,12},{12,8},{16,20},{20,16},{24,28},{28,24},{1,5},{5... | collective-permute-start | bytes 1253384 | tf_op jit(solution)/shard_map/ppermute | solution.py:318
  45.4 15.1 %collective-permute-start.21 = (bf16[256,1024]{1,0:T(8,128)(2,1)}, bf16[256,1024]{1,0:T(8,128)(2,1)S(1)}, u32[]{:S(2)}, u32[]{:S(2)}) collective-permute-start(bf16[256,1024]{1,0:T(8,128)(2,1)} %get-tuple-element.41), channel_id=1, source_target_pairs={{0,8},{4,12},{8,0},{12,4},{16,24},{20,28},{24,16},{28,20},{1,9},{5... | collective-permute-start | bytes 1572872 | tf_op jit(solution)/shard_map/ppermute | solution.py:315
  47.0 25.5 %collective-permute-start.22 = (bf16[256,1024]{1,0:T(8,128)(2,1)}, bf16[256,1024]{1,0:T(8,128)(2,1)S(1)}, u32[]{:S(2)}, u32[]{:S(2)}) collective-permute-start(bf16[256,1024]{1,0:T(8,128)(2,1)} %get-tuple-element.42), channel_id=1, source_target_pairs={{0,16},{4,20},{8,24},{12,28},{16,0},{20,4},{24,8},{28,12},{1,17},{... | collective-permute-start | bytes 1572872 | tf_op jit(solution)/shard_map/ppermute | solution.py:315
  53.9 18.6 %collective-permute-start.23 = (bf16[256,1024]{1,0:T(8,128)(2,1)}, bf16[256,1024]{1,0:T(8,128)(2,1)S(1)}, u32[]{:S(2)}, u32[]{:S(2)}) collective-permute-start(bf16[256,1024]{1,0:T(8,128)(2,1)} %shard_map.85), channel_id=1, source_target_pairs={{0,24},{4,28},{8,16},{12,20},{16,8},{20,12},{24,0},{28,4},{1,25},{... | collective-permute-start | bytes 1572872 | tf_op jit(solution)/shard_map/ppermute | solution.py:315
  55.4 25.9 %collective-permute-start.3 = (bf16[256,1024]{1,0:T(8,128)(2,1)}, bf16[256,1024]{1,0:T(8,128)(2,1)}, u32[]{:S(2)}, u32[]{:S(2)}) collective-permute-start(bf16[256,1024]{1,0:T(8,128)(2,1)} %collective-permute-done.2.refs_2_), channel_id=1, source_target_pairs={{1,0},{2,3},{5,4},{6,7},{9,8},{10,11},{13,12},{14,15},{17,16},{18,... | collective-permute-start | bytes 1572872 | tf_op jit(solution)/shard_map/ppermute | solution.py:330
  56.7 26.9 %collective-permute-start.5 = (bf16[256,1024]{1,0:T(8,128)(2,1)}, bf16[256,1024]{1,0:T(8,128)(2,1)}, u32[]{:S(2)}, u32[]{:S(2)}) collective-permute-start(bf16[256,1024]{1,0:T(8,128)(2,1)} %collective-permute-done.4.refs_4_), channel_id=1, source_target_pairs={{1,0},{2,3},{5,4},{6,7},{9,8},{10,11},{13,12},{14,15},{17,16},{18,... | collective-permute-start | bytes 1572872 | tf_op jit(solution)/shard_map/ppermute | solution.py:330
  60.5 30.0 %collective-permute-start.35 = (bf16[136,1536]{1,0:T(8,128)(2,1)S(1)}, bf16[136,1536]{1,0:T(8,128)(2,1)}, u32[]{:S(2)}, u32[]{:S(2)}) collective-permute-start(bf16[136,1536]{1,0:T(8,128)(2,1)S(1)} %copy-done.5), channel_id=1, source_target_pairs={{0,4},{4,0},{8,12},{12,8},{16,20},{20,16},{24,28},{28,24},{1,5},{5... | collective-permute-start | bytes 1253384 | tf_op jit(solution)/shard_map/ppermute | solution.py:318
  72.5 18.7 %collective-permute-start.38 = (bf16[136,1536]{1,0:T(8,128)(2,1)S(1)}, bf16[136,1536]{1,0:T(8,128)(2,1)}, u32[]{:S(2)}, u32[]{:S(2)}) collective-permute-start(bf16[136,1536]{1,0:T(8,128)(2,1)S(1)} %copy-done.7), channel_id=1, source_target_pairs={{0,4},{4,0},{8,12},{12,8},{16,20},{20,16},{24,28},{28,24},{1,5},{5... | collective-permute-start | bytes 1253384 | tf_op jit(solution)/shard_map/ppermute | solution.py:318
  72.5 18.7 %collective-permute-start.36 = (bf16[136,1536]{1,0:T(8,128)(2,1)}, bf16[136,1536]{1,0:T(8,128)(2,1)}, u32[]{:S(2)}, u32[]{:S(2)}) collective-permute-start(bf16[136,1536]{1,0:T(8,128)(2,1)} %collective-permute-done.9.refs_5_.refs_1_.refs_11_.refs_27_), channel_id=1, source_target_pairs={{0,4},{4,0},{8,12},{12,8},{16,20},{20,16},{24,28},{28,24},{1,5},{5... | collective-permute-start | bytes 1253384 | tf_op jit(solution)/shard_map/ppermute | solution.py:318
  83.6 15.5 %collective-permute-start.24 = (bf16[256,1024]{1,0:T(8,128)(2,1)}, bf16[256,1024]{1,0:T(8,128)(2,1)S(1)}, u32[]{:S(2)}, u32[]{:S(2)}) collective-permute-start(bf16[256,1024]{1,0:T(8,128)(2,1)} %shard_map.86), channel_id=1, source_target_pairs={{0,1},{3,2},{4,5},{7,6},{8,9},{11,10},{12,13},{15,14},{16,17},{19,... | collective-permute-start | bytes 1572872 | tf_op jit(solution)/shard_map/ppermute | solution.py:330
  90.5 15.2 %collective-permute-start.6 = (bf16[256,1024]{1,0:T(8,128)(2,1)}, bf16[256,1024]{1,0:T(8,128)(2,1)}, u32[]{:S(2)}, u32[]{:S(2)}) collective-permute-start(bf16[256,1024]{1,0:T(8,128)(2,1)} %get-tuple-element.29), channel_id=1, source_target_pairs={{0,8},{4,12},{8,0},{12,4},{16,24},{20,28},{24,16},{28,20},{1,9},{5... | collective-permute-start | bytes 1572872 | tf_op jit(solution)/shard_map/ppermute | solution.py:315
  91.2 14.6 %collective-permute-start.40 = (bf16[136,1536]{1,0:T(8,128)(2,1)}, bf16[136,1536]{1,0:T(8,128)(2,1)S(1)}, u32[]{:S(2)}, u32[]{:S(2)}) collective-permute-start(bf16[136,1536]{1,0:T(8,128)(2,1)} %collective-permute-done.15.refs_3_.refs_1_.refs_15_.refs_31_), channel_id=1, source_target_pairs={{0,4},{4,0},{8,12},{12,8},{16,20},{20,16},{24,28},{28,24},{1,5},{5... | collective-permute-start | bytes 1253384 | tf_op jit(solution)/shard_map/ppermute | solution.py:318
  91.2 25.9 %collective-permute-start.7 = (bf16[256,1024]{1,0:T(8,128)(2,1)}, bf16[256,1024]{1,0:T(8,128)(2,1)}, u32[]{:S(2)}, u32[]{:S(2)}) collective-permute-start(bf16[256,1024]{1,0:T(8,128)(2,1)} %get-tuple-element.30), channel_id=1, source_target_pairs={{0,16},{4,20},{8,24},{12,28},{16,0},{20,4},{24,8},{28,12},{1,17},{... | collective-permute-start | bytes 1572872 | tf_op jit(solution)/shard_map/ppermute | solution.py:315
  92.3 26.0 %collective-permute-start.13 = (bf16[256,1024]{1,0:T(8,128)(2,1)}, bf16[256,1024]{1,0:T(8,128)(2,1)}, u32[]{:S(2)}, u32[]{:S(2)}) collective-permute-start(bf16[256,1024]{1,0:T(8,128)(2,1)} %get-tuple-element.33), channel_id=1, source_target_pairs={{0,24},{4,28},{8,16},{12,20},{16,8},{20,12},{24,0},{28,4},{1,25},{... | collective-permute-start | bytes 1572872 | tf_op jit(solution)/shard_map/ppermute | solution.py:315
  99.1 19.4 %collective-permute-start.29 = (bf16[256,1024]{1,0:T(8,128)(2,1)}, bf16[256,1024]{1,0:T(8,128)(2,1)}, u32[]{:S(2)}, u32[]{:S(2)}) collective-permute-start(bf16[256,1024]{1,0:T(8,128)(2,1)} %get-tuple-element.25.refs_0_.refs_1_), channel_id=1, source_target_pairs={{0,4},{4,0},{8,12},{12,8},{16,20},{20,16},{24,28},{28,24},{1,5},{5... | collective-permute-start | bytes 1572872 | tf_op jit(solution)/shard_map/ppermute | solution.py:318
  105.7 20.0 %collective-permute-start.30 = (bf16[256,1024]{1,0:T(8,128)(2,1)}, bf16[256,1024]{1,0:T(8,128)(2,1)S(1)}, u32[]{:S(2)}, u32[]{:S(2)}) collective-permute-start(bf16[256,1024]{1,0:T(8,128)(2,1)} %collective-permute-done.6.refs_0_.refs_1_), channel_id=1, source_target_pairs={{0,4},{4,0},{8,12},{12,8},{16,20},{20,16},{24,28},{28,24},{1,5},{5... | collective-permute-start | bytes 1572872 | tf_op jit(solution)/shard_map/ppermute | solution.py:318
  105.7 21.2 %collective-permute-start.25 = (bf16[256,1024]{1,0:T(8,128)(2,1)}, bf16[256,1024]{1,0:T(8,128)(2,1)S(1)}, u32[]{:S(2)}, u32[]{:S(2)}) collective-permute-start(bf16[256,1024]{1,0:T(8,128)(2,1)} %get-tuple-element.43), channel_id=1, source_target_pairs={{2,1},{1,2},{6,5},{5,6},{10,9},{9,10},{14,13},{13,14},{18,17},{17,... | collective-permute-start | bytes 1572872 | tf_op jit(solution)/shard_map/ppermute | solution.py:330
  117.0 19.2 %collective-permute-start.26 = (bf16[256,1024]{1,0:T(8,128)(2,1)}, bf16[256,1024]{1,0:T(8,128)(2,1)S(1)}, u32[]{:S(2)}, u32[]{:S(2)}) collective-permute-start(bf16[256,1024]{1,0:T(8,128)(2,1)} %get-tuple-element.44), channel_id=1, source_target_pairs={{0,1},{3,2},{4,5},{7,6},{8,9},{11,10},{12,13},{15,14},{16,17},{19,... | collective-permute-start | bytes 1572872 | tf_op jit(solution)/shard_map/ppermute | solution.py:330
  118.4 24.3 %collective-permute-start.31 = (bf16[256,1024]{1,0:T(8,128)(2,1)}, bf16[256,1024]{1,0:T(8,128)(2,1)}, u32[]{:S(2)}, u32[]{:S(2)}) collective-permute-start(bf16[256,1024]{1,0:T(8,128)(2,1)} %collective-permute-done.7.refs_2_.refs_3_), channel_id=1, source_target_pairs={{0,4},{4,0},{8,12},{12,8},{16,20},{20,16},{24,28},{28,24},{1,5},{5... | collective-permute-start | bytes 1572872 | tf_op jit(solution)/shard_map/ppermute | solution.py:318
  118.5 25.1 %collective-permute-start.32 = (bf16[256,1024]{1,0:T(8,128)(2,1)}, bf16[256,1024]{1,0:T(8,128)(2,1)}, u32[]{:S(2)}, u32[]{:S(2)}) collective-permute-start(bf16[256,1024]{1,0:T(8,128)(2,1)} %collective-permute-done.13.refs_0_.refs_1_.refs_3_), channel_id=1, source_target_pairs={{0,4},{4,0},{8,12},{12,8},{16,20},{20,16},{24,28},{28,24},{1,5},{5... | collective-permute-start | bytes 1572872 | tf_op jit(solution)/shard_map/ppermute | solution.py:318
  139.4 33.6 %collective-permute-start.27 = (bf16[256,1024]{1,0:T(8,128)(2,1)}, bf16[256,1024]{1,0:T(8,128)(2,1)S(1)}, u32[]{:S(2)}, u32[]{:S(2)}) collective-permute-start(bf16[256,1024]{1,0:T(8,128)(2,1)} %get-tuple-element.45), channel_id=1, source_target_pairs={{1,0},{0,1},{3,2},{2,3},{5,4},{4,5},{7,6},{6,7},{9,8},{8,9},{11,10... | collective-permute-start | bytes 1572872 | tf_op jit(solution)/shard_map/ppermute | solution.py:330
  139.5 33.5 %collective-permute-start.28 = (bf16[256,1024]{1,0:T(8,128)(2,1)}, bf16[256,1024]{1,0:T(8,128)(2,1)S(1)}, u32[]{:S(2)}, u32[]{:S(2)}) collective-permute-start(bf16[256,1024]{1,0:T(8,128)(2,1)} %get-tuple-element.46), channel_id=1, source_target_pairs={{2,1},{1,2},{6,5},{5,6},{10,9},{9,10},{14,13},{13,14},{18,17},{17,... | collective-permute-start | bytes 1572872 | tf_op jit(solution)/shard_map/ppermute | solution.py:330
  142.7 27.5 %collective-permute-start.20 = (bf16[128,1536]{1,0:T(8,128)(2,1)}, bf16[128,1536]{1,0:T(8,128)(2,1)}, u32[]{:S(2)}, u32[]{:S(2)}) collective-permute-start(bf16[128,1536]{1,0:T(8,128)(2,1)} %get-tuple-element.40), channel_id=1, source_target_pairs={{0,16},{4,20},{8,24},{12,28},{16,0},{20,4},{24,8},{28,12},{1,17},{... | collective-permute-start | bytes 1179656 | tf_op jit(solution)/shard_map/ppermute | solution.py:315
  143.6 26.6 %collective-permute-start.18 = (bf16[128,1536]{1,0:T(8,128)(2,1)}, bf16[128,1536]{1,0:T(8,128)(2,1)}, u32[]{:S(2)}, u32[]{:S(2)}) collective-permute-start(bf16[128,1536]{1,0:T(8,128)(2,1)} %get-tuple-element.37), channel_id=1, source_target_pairs={{0,16},{4,20},{8,24},{12,28},{16,0},{20,4},{24,8},{28,12},{1,17},{... | collective-permute-start | bytes 1179656 | tf_op jit(solution)/shard_map/ppermute | solution.py:315
  147.1 23.1 %collective-permute-start.19 = (bf16[128,1536]{1,0:T(8,128)(2,1)}, bf16[128,1536]{1,0:T(8,128)(2,1)}, u32[]{:S(2)}, u32[]{:S(2)}) collective-permute-start(bf16[128,1536]{1,0:T(8,128)(2,1)} %get-tuple-element.39), channel_id=1, source_target_pairs={{0,8},{4,12},{8,0},{12,4},{16,24},{20,28},{24,16},{28,20},{1,9},{5... | collective-permute-start | bytes 1179656 | tf_op jit(solution)/shard_map/ppermute | solution.py:315
  (23 other events, 329.8 us)
where the time goes:
time: 175 us; the launch traced here: 174 us
  Pallas kernels  75.7 us (43%)
  waiting for transfers between devices  55.1 us (31%)
  starting transfers between devices  40.3 us (23%)
    ppermute x18, waiting for transfers between devices, across(): return lax.ppermute(value, 'loop', pairs)  47.5 us
    ppermute x18, starting transfers between devices, across(): return lax.ppermute(value, 'loop', pairs)  24.5 us
    pallas_call x3, Pallas kernels, project_parts(): pl.pallas_call(functools.partial(project_kernel, items=len(items)), grid_...  22 us
    pallas_call x3, Pallas kernels, input_terms(): pl.pallas_call(functools.partial(input_kernel, blocks=len(blocks), tile=t...  22 us
    pallas_call x1, Pallas kernels, weight_gradient(): pl.pallas_call(functools.partial(weight_kernel, blocks=len(blocks), grads...  15.1 us
    ppermute x10, starting transfers between devices, along(): return lax.ppermute(value, 'tp', pairs)  14 us
    pallas_call x5, Pallas kernels, fold(): pl.pallas_call(functools.partial(fold_kernel, sources=len(sources), count...  8.9 us
    ppermute x10, waiting for transfers between devices, along(): return lax.ppermute(value, 'tp', pairs)  7.08 us
  transfers between devices with their start and end apart: 41, of which 11 were waited for; matrix products, arithmetic and copies ran while one was open for 0% of the time, Pallas kernels for 43%

commit v1 on v0

--- a/solution.py
+++ b/solution.py
@@ -12,39 +12,80 @@
 BF16 = jnp.bfloat16
 F32 = jnp.float32
 KIND_ROWS = 8
+PART_KINDS = ((0, 1), (2, 1))
 PROJECT_TILE = 512
 WEIGHT_TILE = 512
 
 
-def pack_kernel(kinds_of_loops, dest, grads, *outs, capacity):
+def placing(place, dtype=BF16):
+    count = place.shape[1]
+    rows = lax.broadcasted_iota(jnp.int32, (count, count), 0)
+    return (rows == place.astype(jnp.int32)).astype(F32).astype(dtype)
+
+
+def pack_kernel(kinds_of_loops, dest, grads, first, second, places, *, capacity, kinds):
     slots = dest[...]
     found = jnp.full(slots.shape, kinds_of_loops[0], jnp.int32)
     for loop_index in range(1, kinds_of_loops.shape[0]):
         found = jnp.where(slots >= loop_index * capacity, kinds_of_loops[loop_index], found)
-    cut = slots.shape[1] // len(outs)
-    for part, out in enumerate(outs):
+    count = slots.shape[1]
+    upto = lax.broadcasted_iota(jnp.int32, (count, count), 0) <= lax.broadcasted_iota(jnp.int32, (count, count), 1)
+    upto = upto.astype(F32).astype(BF16)
+    lane = lax.broadcasted_iota(jnp.int32, (1, count), 1).astype(F32)
+    place = jnp.zeros((1, count), F32)
+    kind = jnp.zeros((1, count), F32)
+    start = jnp.zeros((1, 1), F32)
+    for which in range(kinds):
+        mine = (found == which).astype(F32)
+        counted = jnp.dot(
+            jnp.broadcast_to(mine, (8, count)).astype(BF16), upto, preferred_element_type=F32
+        )[:1]
+        place = place + mine * (start + counted - 1.0)
+        if which:
+            kind = kind + (lane >= start).astype(F32)
+        start = start + jnp.sum(mine, axis=1, keepdims=True)
+    places[...] = jnp.broadcast_to(place, places.shape)
+    ordered = jnp.dot(placing(place), grads[...], preferred_element_type=F32).astype(BF16)
+    cut = count // 2
+    for part, out in enumerate((first, second)):
         extra = out.shape[0] - cut
-        kind = found[:, part * cut:(part + 1) * cut].astype(F32).astype(BF16)
-        out[:cut] = grads[part * cut:(part + 1) * cut]
+        out[:cut] = ordered[part * cut:(part + 1) * cut]
         out[cut:] = jnp.zeros((extra, out.shape[1]), BF16)
-        out[cut:, :cut] = jnp.broadcast_to(kind, (extra, cut))
-
-
-def packed_grads(out_grad, dest_row, loop_modality, capacity):
+        out[cut:, :cut] = jnp.broadcast_to(kind[:, part * cut:(part + 1) * cut], (extra, cut)).astype(BF16)
+
+
+def packed_grads(out_grad, dest_row, loop_modality, capacity, kinds):
     rows, columns = out_grad.shape
     slots = dest_row.reshape(1, -1)
     packed = (rows // 2 + KIND_ROWS, columns)
     return pl.pallas_call(
-        functools.partial(pack_kernel, capacity=capacity),
+        functools.partial(pack_kernel, capacity=capacity, kinds=kinds),
         grid_spec=pltpu.PrefetchScalarGridSpec(
             num_scalar_prefetch=1,
             grid=(1,),
             in_specs=[whole(slots.shape), whole(out_grad.shape)],
-            out_specs=[whole(packed), whole(packed)],
+            out_specs=[whole(packed), whole(packed), whole((8, rows))],
         ),
-        out_shape=[pltpu.HBM(packed, BF16)] * 2,
-        compiler_params=limit(8),
+        out_shape=[
+            jax.ShapeDtypeStruct(packed, BF16), jax.ShapeDtypeStruct(packed, BF16), pltpu.HBM((8, rows), F32)
+        ],
+        compiler_params=limit(60),
     )(loop_modality, *in_hbm(slots, out_grad))
+
+
+def sort_kernel(places, rows, out):
+    out[...] = jnp.dot(placing(places[:1]), rows[...], preferred_element_type=F32).astype(BF16)
+
+
+def sorted_rows(places, rows):
+    return pl.pallas_call(
+        sort_kernel,
+        grid=(1,),
+        in_specs=[whole(places.shape), whole(rows.shape)],
+        out_specs=whole(rows.shape),
+        out_shape=pltpu.HBM(rows.shape, BF16),
+        compiler_params=limit(16),
+    )(*in_hbm(places, rows))
 
 
 def in_hbm(*values):
@@ -60,45 +101,35 @@
     return pl.BlockSpec((KIND_ROWS, cut), lambda *_: (cut // KIND_ROWS, 0))
 
 
-def pick(kind, products):
-    chosen = products[0]
-    for index in range(1, len(products)):
-        chosen = jnp.where(kind == index, products[index], chosen)
-    return chosen
-
-
 def whole(shape):
     return pl.BlockSpec(shape, lambda *_: (0,) * len(shape))
 
 
-def split_rows(value, outs):
-    start = 0
-    for out in outs:
-        yield out, value[start:start + out.shape[0]]
-        start += out.shape[0]
-
-
 def limit(mebibytes):
     return pltpu.CompilerParams(vmem_limit_bytes=mebibytes << 20)
 
 
 def input_kernel(core, own_weight, other_weight, *refs, blocks, tile):
     cut = refs[0].shape[0] - KIND_ROWS
-    rhs = jnp.concatenate([ref[:cut] for ref in refs[:blocks]], axis=0)
-    kind = kinds_in([ref[cut:, :cut] for ref in refs[:blocks]])
+    halves = [refs[part:blocks:2] for part in (0, 1)]
+    sides = [jnp.concatenate([ref[:cut] for ref in some], axis=0) for some in halves]
+    kinds = [kinds_in([ref[cut:, :cut] for ref in some]) for some in halves]
     outs = refs[blocks:]
     half = outs[0].shape[1] // 2
-    kinds, _, columns = own_weight.shape
+
+    def product(weight, rows):
+        return lax.dot_general(weight, rows, (((1,), (1,)), ((), ())), preferred_element_type=F32)
+
     for weight, side in ((own_weight, core[0]), (other_weight, 1 - core[0])):
-        product = lax.dot_general(
-            weight[...].reshape(kinds * tile, columns), rhs, (((1,), (1,)), ((), ())),
-            preferred_element_type=F32,
-        )
-        products = [product[index * tile:(index + 1) * tile] for index in range(kinds)]
-        chosen = pick(kind, products).astype(BF16).T
+        common = product(weight[1], jnp.concatenate(sides, axis=0))
         at = pl.multiple_of(side * half + pl.program_id(0) * tile, tile)
-        for out, part in split_rows(chosen, outs):
-            out[:, pl.ds(at, tile)] = part
+        span = sides[0].shape[0]
+        for part, (special, _) in enumerate(PART_KINDS):
+            mine = product(weight[special], sides[part])
+            chosen = jnp.where(kinds[part] == special, mine, common[:, part * span:(part + 1) * span])
+            chosen = chosen.astype(BF16).T
+            for number, out in enumerate(outs):
+                out[part * cut:(part + 1) * cut, pl.ds(at, tile)] = chosen[number * cut:(number + 1) * cut]
 
 
 def input_terms(core, blocks, sizes, own_weight, other_weight):
@@ -126,14 +157,22 @@
     other = jnp.concatenate([ref[:, pl.ds(other_at, half)] for ref in refs[:items]], axis=0)
     kind = kinds_in([ref[...] for ref in refs[items:2 * items]])
     row_kind = jnp.broadcast_to(kind, (tile, kind.shape[1])).T
-    products = [
-        jnp.dot(own, own_weight[index], preferred_element_type=F32)
-        + jnp.dot(other, other_weight[index], preferred_element_type=F32)
-        for index in range(own_weight.shape[0])
-    ]
-    chosen = pick(row_kind, products).astype(BF16)
-    for out, part in split_rows(chosen, refs[2 * items:]):
-        out[...] = part
+    outs = refs[2 * items:]
+
+    def product(which, rows):
+        return (
+            jnp.dot(own[rows], own_weight[which], preferred_element_type=F32)
+            + jnp.dot(other[rows], other_weight[which], preferred_element_type=F32)
+        )
+
+    span = own.shape[0] // 2
+    cut = outs[0].shape[0]
+    common = product(1, slice(None))
+    for part, (special, _) in enumerate(PART_KINDS):
+        rows = slice(part * span, (part + 1) * span)
+        chosen = jnp.where(row_kind[rows] == special, product(special, rows), common[rows]).astype(BF16)
+        for number in range(items // 2):
+            outs[part * (items // 2) + number][...] = chosen[number * cut:(number + 1) * cut]
 
 
 def project_parts(core, items, own_weight, other_weight):
@@ -179,26 +218,30 @@
     )(*in_hbm(*values))
 
 
-def finish_kernel(*refs, count):
-    out = refs[-1]
-    cut = out.shape[0] // 2
+def finish_kernel(places, term, *refs, count):
+    projected, input_grad = refs[-2:]
+    sums = []
     for part in (0, 1):
         total = refs[part * count][...].astype(F32)
         for ref in refs[part * count + 1:(part + 1) * count]:
             total = total + ref[...].astype(F32)
-        out[part * cut:(part + 1) * cut] = total.astype(BF16)
-
-
-def finish(first, second):
+        sums.append(total.astype(BF16))
+    back = placing(places[:1], F32).T.astype(BF16)
+    projected[...] = jnp.dot(back, jnp.concatenate(sums, axis=0), preferred_element_type=F32).astype(BF16)
+    input_grad[...] = jnp.dot(back, term[...], preferred_element_type=F32).astype(BF16)
+
+
+def finish(places, term, first, second):
     cut, columns = first[0].shape
+    shapes = ((2 * cut, columns), term.shape)
     return pl.pallas_call(
         functools.partial(finish_kernel, count=len(first)),
         grid=(1,),
-        in_specs=[whole((cut, columns))] * (2 * len(first)),
-        out_specs=whole((2 * cut, columns)),
-        out_shape=jax.ShapeDtypeStruct((2 * cut, columns), BF16),
-        compiler_params=limit(16),
-    )(*in_hbm(*first, *second))
+        in_specs=[whole(places.shape), whole(term.shape)] + [whole((cut, columns))] * (2 * len(first)),
+        out_specs=[whole(shape) for shape in shapes],
+        out_shape=[jax.ShapeDtypeStruct(shape, BF16) for shape in shapes],
+        compiler_params=limit(20),
+    )(*in_hbm(places), term, *in_hbm(*first, *second))
 
 
 def fold_kernel(wanted, *refs, sources, counts):
@@ -247,25 +290,26 @@
     rows = refs[:blocks]
     columns_of = refs[blocks:blocks + grads]
     kind_rows = refs[blocks + grads:blocks + 2 * grads]
-    out, turned = refs[blocks + 2 * grads:]
-    kinds, _, _ = out.shape
+    out, *turned = refs[blocks + 2 * grads:]
 
     @pl.when(pl.program_id(0) == 0)
     def _():
-        kind = kinds_in([ref[...] for ref in kind_rows])
-        start = 0
-        for ref in rows:
-            count = ref.shape[0]
-            part = ref[...].T
-            own_kind = kind[:, start:start + count]
-            for which in range(kinds):
-                turned[which, :, start:start + count] = jnp.where(own_kind == which, part, 0)
-            start += count
-
-    columns = jnp.concatenate([ref[...] for ref in columns_of], axis=0)
-    for which in range(kinds):
-        total = jnp.dot(turned[which], columns, preferred_element_type=F32)
-        out[which] = (total * scale).astype(BF16)
+        for number, ref in enumerate(rows):
+            cut = ref.shape[0] // 2
+            block = ref[...].T
+            for part, part_kinds in enumerate(PART_KINDS):
+                own_kind = kind_rows[2 * number + part][:1].astype(F32)
+                for place, which in enumerate(part_kinds):
+                    turned[part][place, :, number * cut:(number + 1) * cut] = jnp.where(
+                        own_kind == which, block[:, part * cut:(part + 1) * cut], 0
+                    )
+
+    columns = [jnp.concatenate([ref[...] for ref in columns_of[part::2]], axis=0) for part in (0, 1)]
+    common = sum(jnp.dot(turned[part][1], columns[part], preferred_element_type=F32) for part in (0, 1))
+    out[1] = (common * scale).astype(BF16)
+    for part, (special, _) in enumerate(PART_KINDS):
+        total = jnp.dot(turned[part][0], columns[part], preferred_element_type=F32)
+        out[special] = (total * scale).astype(BF16)
 
 
 def weight_gradient(core, blocks, half_blocks, kinds, scale):
@@ -283,7 +327,7 @@
             + [pl.BlockSpec((cut, tile), lambda step, core: (0, step)) for _ in half_blocks]
             + [kind_spec(block) for block in half_blocks],
             out_specs=pl.BlockSpec((kinds, half, tile), lambda step, core: (0, 0, step)),
-            scratch_shapes=[pltpu.VMEM((kinds, half, rows * len(blocks)), BF16)],
+            scratch_shapes=[pltpu.VMEM((2, half, rows // 2 * len(blocks)), BF16)] * 2,
         ),
         out_shape=jax.ShapeDtypeStruct((kinds, half, columns), BF16),
         compiler_params=limit(36),
@@ -309,6 +353,7 @@
     bits = [1 << place for place in range(chip_count.bit_length() - 1)]
     offsets = sorted(range(1, chip_count), key=lambda offset: (bin(offset).count("1"), offset))
     several = [offset for offset in offsets if offset & (offset - 1)]
+    cut = row_count // 2
 
     def across(value, offset):
         pairs = [(i, i ^ (2 * offset)) for i in range(loop_count)]
@@ -332,7 +377,10 @@
     stages = range(1, tp_count)
     facing = [jnp.where(level % 2 == parity, 1, -1) for parity in (0, 1)]
 
+    assert kinds == 3 and capacity * loop_count // 4 <= cut
     other_weight = sibling(qkv_weight)
+    *own_grad, order = packed_grads(out_grad, dest_row, loop_modality, capacity, kinds)
+    tokens = sorted_rows(order, tokens)
     came = {(0, 0): tokens, (1, 0): tokens}
     for stage in stages:
         for parity in (0, 1):
@@ -340,7 +388,6 @@
             if pairs:
                 came[parity, stage] = along(came[1 - parity, stage - 1], pairs)
 
-    own_grad = packed_grads(out_grad, dest_row, loop_modality, capacity)
     grads = {0: own_grad}
     for bit in bits:
         grads[bit] = [None, None]
@@ -375,7 +422,7 @@
             pairs = [(b, a) for a, b in line_pairs(parity, stage)]
             back[parity, stage] = along(value, pairs)
     last = [back[parity, 1] for parity in (0, 1) if (parity, 1) in back]
-    input_grad = fold([term_number(level)], all_terms, [last])[0]
+    own_input = fold([term_number(level)], all_terms, [last])[0]
 
     places = [place for place in came if place != (1, 0)]
     sources = [came[place] for place in places]
@@ -393,6 +440,7 @@
     pieces = {(offset, part): [] for offset in range(chip_count) for part in (0, 1)}
 
     def project(places):
+        places = sorted(places, key=lambda place: place[1])
         items = [(rows[offset], part, grads[offset][part]) for offset, part in places]
         made = project_parts(core, items, qkv_weight, other_weight)
         return dict(zip(places, made))
@@ -409,7 +457,7 @@
             link = offset if offset in bits else low_high(offset)[part]
             piece = across(made[offset, part], link)
             pieces[offset ^ link, part].append(piece)
-    projected = finish([own_parts[0, 0], *pieces[0, 0]], [own_parts[0, 1], *pieces[0, 1]])
+    projected, input_grad = finish(order, own_input, [own_parts[0, 0], *pieces[0, 0]], [own_parts[0, 1], *pieces[0, 1]])
 
     near = [rows[offset] for offset in range(chip_count)]
     far = [sibling(block) for block in near]

time: 175 us -> 161 us (0.920)
  waiting for transfers between devices: 55.1 us -> 39.3 us
  Pallas kernels: 75.7 us -> 71.9 us
  starting transfers between devices: 40.3 us -> 43.2 us
  local copies, waits for them, and re-layouts: 1.74 us -> 3.92 us
    ppermute x18, waiting for transfers between devices: 47.5 us -> 30.6 us  [across(): return lax.ppermute(value, 'loop', pairs)]
    ppermute x10, starting transfers between devices: 14 us -> 19.4 us  [along(): return lax.ppermute(value, 'tp', pairs)]
    ppermute x18, starting transfers between devices: 24.5 us -> 21.1 us  [across(): return lax.ppermute(value, 'loop', pairs)]
    pallas_call x1, Pallas kernels: 15.1 us -> 12 us  [weight_gradient(): pl.pallas_call(functools.partial(weight_kernel, blocks=len(blocks), grads...]
    pallas_call x1 -> x2, Pallas kernels: 2.65 us -> 5.37 us  [the longest x1 3.23 us: packed_grads(): pl.pallas_call(functools.partial(pack_kernel, capacity=capacity, kinds=ki...]
    unnamed x28 -> x38, local copies, waits for them, and re-layouts: 1.74 us -> 3.92 us
    pallas_call x3, Pallas kernels: 22 us -> 19.8 us  [project_parts(): pl.pallas_call(functools.partial(project_kernel, items=len(items)), grid_...]
where the time goes in v1:
time: 161 us; the launch traced here: 160 us
  Pallas kernels  71.9 us (45%)
  starting transfers between devices  43.2 us (27%)
  waiting for transfers between devices  39.3 us (24%)
  local copies, waits for them, and re-layouts  3.92 us (2%)
    ppermute x18, waiting for transfers between devices, across(): return lax.ppermute(value, 'loop', pairs)  30.6 us
    ppermute x18, starting transfers between devices, across(): return lax.ppermute(value, 'loop', pairs)  21.1 us
    pallas_call x3, Pallas kernels, input_terms(): pl.pallas_call(functools.partial(input_kernel, blocks=len(blocks), tile=t...  20.3 us
    pallas_call x3, Pallas kernels, project_parts(): pl.pallas_call(functools.partial(project_kernel, items=len(items)), grid_...  19.8 us
    ppermute x10, starting transfers between devices, along(): return lax.ppermute(value, 'tp', pairs)  19.4 us
    pallas_call x1, Pallas kernels, weight_gradient(): pl.pallas_call(functools.partial(weight_kernel, blocks=len(blocks), grads...  12 us
    pallas_call x5, Pallas kernels, fold(): pl.pallas_call(functools.partial(fold_kernel, sources=len(sources), count...  8.86 us
    ppermute x10, waiting for transfers between devices, along(): return lax.ppermute(value, 'tp', pairs)  8.68 us
  transfers between devices with their start and end apart: 41, of which 11 were waited for; matrix products, arithmetic and copies ran while one was open for 0% of the time, Pallas kernels for 43%

profile of v1, /device:TPU:0, one launch (start us, length us, event | category | flops | bytes accessed | tf_op | source)
XLA Modules:
  0.0 159.6 jit_solution(16531933843607391610)
XLA Ops:
  1.2 3.2 %shard_map.76 = (bf16[136,1536]{1,0:T(8,128)(2,1)}, bf16[136,1536]{1,0:T(8,128)(2,1)}, f32[8,256]{1,0:T(8,128)}) custom-call(s32[8]{0:T(128)} %kinds_of_loops.1, s32[1,256]{1,0:T(1,128)} %bitcast.12, bf16[256,1536]{1,0:T(8,128)(2,1)} %grads.1), custom_call_target="tpu_custom_call" | custom-call | tf_op jit(solution)/shard_map/pallas_call | solution.py:61
  4.4 2.5 %collective-permute-start.3 = (bf16[136,1536]{1,0:T(8,128)(2,1)}, bf16[136,1536]{1,0:T(8,128)(2,1)S(1)}, u32[]{:S(2)}, u32[]{:S(2)}) collective-permute-start(bf16[136,1536]{1,0:T(8,128)(2,1)} %get-tuple-element.29.refs_0_.refs_2_.refs_8_.refs_24_), channel_id=1, source_target_pairs={{0,16},{4,20},{8,24},{12,28},{16,0},{20,4},{24,8},{28,12},{1,17},{... | collective-permute-start | bytes 1253384 | tf_op jit(solution)/shard_map/ppermute | solution.py:360
  6.9 2.1 %shard_map.84.refs_0_ = bf16[256,1024]{1,0:T(8,128)(2,1)} custom-call(f32[8,256]{1,0:T(8,128)} %get-tuple-element.28.places, bf16[256,1024]{1,0:T(8,128)(2,1)} %rows.1), custom_call_target="tpu_custom_call" | custom-call | tf_op jit(solution)/shard_map/pallas_call | solution.py:81
  9.1 1.6 collective-permute-start.15
  10.7 1.5 collective-permute-start.1
  12.7 5.0 %collective-permute-done.3.refs_2_.refs_5_.refs_12_.refs_28_ = bf16[136,1536]{1,0:T(8,128)(2,1)S(1)} collective-permute-done((bf16[136,1536]{1,0:T(8,128)(2,1)}, bf16[136,1536]{1,0:T(8,128)(2,1)S(1)}, u32[]{:S(2)}, u32[]{:S(2)}) %collective-permute-start.3) | collective-permute-done | bytes 417824 | tf_op jit(solution)/shard_map/ppermute | solution.py:360
  17.6 2.0 %collective-permute-start.2 = (bf16[136,1536]{1,0:T(8,128)(2,1)}, bf16[136,1536]{1,0:T(8,128)(2,1)S(1)}, u32[]{:S(2)}, u32[]{:S(2)}) collective-permute-start(bf16[136,1536]{1,0:T(8,128)(2,1)} %get-tuple-element.30.refs_1_.refs_3_.refs_9_.refs_25_), channel_id=1, source_target_pairs={{0,8},{4,12},{8,0},{12,4},{16,24},{20,28},{24,16},{28,20},{1,9},{5... | collective-permute-start | bytes 1253384 | tf_op jit(solution)/shard_map/ppermute | solution.py:360
  19.6 3.7 %collective-permute-done.1.refs_0_.refs_4_.refs_10_.refs_26_ = bf16[136,1536]{1,0:T(8,128)(2,1)S(1)} collective-permute-done((bf16[136,1536]{1,0:T(8,128)(2,1)}, bf16[136,1536]{1,0:T(8,128)(2,1)S(1)}, u32[]{:S(2)}, u32[]{:S(2)}) %collective-permute-start.1) | collective-permute-done | bytes 417824 | tf_op jit(solution)/shard_map/ppermute | solution.py:360
  23.4 1.5 collective-permute-start.16
  26.5 1.7 %collective-permute-start.7 = (bf16[136,1536]{1,0:T(8,128)(2,1)S(1)}, bf16[136,1536]{1,0:T(8,128)(2,1)S(1)}, u32[]{:S(2)}, u32[]{:S(2)}) collective-permute-start(bf16[136,1536]{1,0:T(8,128)(2,1)S(1)} %collective-permute-done.3.refs_2_.refs_5_.refs_12_.refs_28_), channel_id=1, source_target_pairs={{0,8},{4,12},{8,0},{12,4},{16,24},{20,28},{24,16},{28,20},{1,9},{5... | collective-permute-start | bytes 1253384 | tf_op jit(solution)/shard_map/ppermute | solution.py:360
  28.2 4.1 %collective-permute-done.2.refs_1_.refs_6_.refs_11_.refs_27_ = bf16[136,1536]{1,0:T(8,128)(2,1)S(1)} collective-permute-done((bf16[136,1536]{1,0:T(8,128)(2,1)}, bf16[136,1536]{1,0:T(8,128)(2,1)S(1)}, u32[]{:S(2)}, u32[]{:S(2)}) %collective-permute-start.2) | collective-permute-done | bytes 417824 | tf_op jit(solution)/shard_map/ppermute | solution.py:360
  33.1 7.7 %shard_map.78 = (bf16[256,1024]{1,0:T(8,128)(2,1)}, bf16[256,1024]{1,0:T(8,128)(2,1)}) custom-call(s32[1]{0:T(128)} %bitcast.2.core, bf16[3,512,1536]{2,1,0:T(8,128)(2,1)} %own_weight.11, bf16[3,512,1536]{2,1,0:T(8,128)(2,1)} %collective-permute-done.other_weight, bf16[136,1536]{1,0:T(8,128)(2,1)} %copy-done.5, bf16[136,1536]{1,0:T(8,128)(2,1)} %copy-done.7, ...), custom_call_target="tpu_custom_call" | custom-call | tf_op jit(solution)/shard_map/pallas_call | solution.py:139
  40.8 1.5 collective-permute-start.5
  44.4 6.3 %shard_map.79 = bf16[256,1024]{1,0:T(8,128)(2,1)} custom-call(s32[1]{0:T(128)} %bitcast.2.core, bf16[3,512,1536]{2,1,0:T(8,128)(2,1)} %own_weight.11, bf16[3,512,1536]{2,1,0:T(8,128)(2,1)} %collective-permute-done.other_weight, bf16[136,1536]{1,0:T(8,128)(2,1)} %copy-done.8, bf16[136,1536]{1,0:T(8,128)(2,1)} %copy-done.9), custom_call_target="tpu_custom_call" | custom-call | tf_op jit(solution)/shard_map/pallas_call | solution.py:139
  54.6 10.7 %collective-permute-done.6.refs_2_ = bf16[256,1024]{1,0:T(8,128)(2,1)S(1)} collective-permute-done((bf16[256,1024]{1,0:T(8,128)(2,1)}, bf16[256,1024]{1,0:T(8,128)(2,1)S(1)}, u32[]{:S(2)}, u32[]{:S(2)}) %collective-permute-start.6) | collective-permute-done | bytes 524320 | tf_op jit(solution)/shard_map/ppermute | solution.py:360
  65.4 6.3 %shard_map.77.refs_0_ = bf16[256,1024]{1,0:T(8,128)(2,1)} custom-call(s32[1]{0:T(128)} %bitcast.2.core, bf16[3,512,1536]{2,1,0:T(8,128)(2,1)} %own_weight.11, bf16[3,512,1536]{2,1,0:T(8,128)(2,1)} %collective-permute-done.other_weight, bf16[136,1536]{1,0:T(8,128)(2,1)} %get-tuple-element.29.refs_0_.refs_2_.refs_8_.refs_24_, ...), custom_call_target="tpu_custom_call" | custom-call | tf_op jit(solution)/shard_map/pallas_call | solution.py:139
  73.6 2.5 %collective-permute-start.10 = (bf16[256,1024]{1,0:T(8,128)(2,1)}, bf16[256,1024]{1,0:T(8,128)(2,1)S(1)}, u32[]{:S(2)}, u32[]{:S(2)}) collective-permute-start(bf16[256,1024]{1,0:T(8,128)(2,1)} %shard_map.80), channel_id=1, source_target_pairs={{0,1},{3,2},{4,5},{7,6},{8,9},{11,10},{12,13},{15,14},{16,17},{19,... | collective-permute-start | bytes 1572872 | tf_op jit(solution)/shard_map/ppermute | solution.py:375
  77.0 3.4 %shard_map.85 = (bf16[256,1024]{1,0:T(8,128)(2,1)}, bf16[256,1024]{1,0:T(8,128)(2,1)}, bf16[256,1024]{1,0:T(8,128)(2,1)}, bf16[256,1024]{1,0:T(8,128)(2,1)}) custom-call(s32[4]{0:T(128)S(1)} %pad_add_fusion.2.wanted, bf16[256,1024]{1,0:T(8,128)(2,1)} %shard_map.84.refs_0_, bf16[256,1024]{1,0:T(8,128)(2,1)} %copy-done.15, ...), custom_call_target="tpu_custom_call" | custom-call | tf_op jit(solution)/shard_map/pallas_call | solution.py:273
  82.1 6.1 %collective-permute-done.10.refs_4_ = bf16[256,1024]{1,0:T(8,128)(2,1)S(1)} collective-permute-done((bf16[256,1024]{1,0:T(8,128)(2,1)}, bf16[256,1024]{1,0:T(8,128)(2,1)S(1)}, u32[]{:S(2)}, u32[]{:S(2)}) %collective-permute-start.10) | collective-permute-done | bytes 524320 | tf_op jit(solution)/shard_map/ppermute | solution.py:375
  88.3 1.7 %shard_map.81 = (bf16[256,1024]{1,0:T(8,128)(2,1)}, bf16[256,1024]{1,0:T(8,128)(2,1)}) custom-call(s32[2]{0:T(128)S(1)} %pad_add_fusion.1.wanted, bf16[256,1024]{1,0:T(8,128)(2,1)S(1)} %copy-done.1, bf16[256,1024]{1,0:T(8,128)(2,1)S(1)} %collective-permute-done.5.refs_1_, bf16[256,1024]{1,0:T(8,128)(2,1)S(1)} %collective-permute-done.6.refs_2_, ...), custom_call_target="tpu_custom_call" | custom-call | tf_op jit(solution)/shard_map/pallas_call | solution.py:273
  91.9 8.2 %collective-permute-start.12 = (bf16[256,1024]{1,0:T(8,128)(2,1)}, bf16[256,1024]{1,0:T(8,128)(2,1)S(1)}, u32[]{:S(2)}, u32[]{:S(2)}) collective-permute-start(bf16[256,1024]{1,0:T(8,128)(2,1)} %get-tuple-element.34), channel_id=1, source_target_pairs={{0,1},{3,2},{4,5},{7,6},{8,9},{11,10},{12,13},{15,14},{16,17},{19,... | collective-permute-start | bytes 1572872 | tf_op jit(solution)/shard_map/ppermute | solution.py:375
  100.2 6.2 %shard_map.88 = (bf16[128,1536]{1,0:T(8,128)(2,1)}, bf16[128,1536]{1,0:T(8,128)(2,1)}) custom-call(s32[1]{0:T(128)} %bitcast.2.core, bf16[3,512,1536]{2,1,0:T(8,128)(2,1)} %own_weight.11, bf16[3,512,1536]{2,1,0:T(8,128)(2,1)} %collective-permute-done.other_weight, bf16[256,1024]{1,0:T(8,128)(2,1)} %collective-permute-done.23.refs_0_.refs_1_.refs_3_, ...), custom_call_target="tpu_custom_call" | custom-call | tf_op jit(solution)/shard_map/pallas_call | solution.py:183
  108.3 2.5 %collective-permute-done.12.refs_5_ = bf16[256,1024]{1,0:T(8,128)(2,1)S(1)} collective-permute-done((bf16[256,1024]{1,0:T(8,128)(2,1)}, bf16[256,1024]{1,0:T(8,128)(2,1)S(1)}, u32[]{:S(2)}, u32[]{:S(2)}) %collective-permute-start.12) | collective-permute-done | bytes 524320 | tf_op jit(solution)/shard_map/ppermute | solution.py:375
  110.9 1.7 %collective-permute-start.25 = (bf16[128,1536]{1,0:T(8,128)(2,1)}, bf16[128,1536]{1,0:T(8,128)(2,1)S(1)}, u32[]{:S(2)}, u32[]{:S(2)}) collective-permute-start(bf16[128,1536]{1,0:T(8,128)(2,1)} %get-tuple-element.46), channel_id=1, source_target_pairs={{0,8},{4,12},{8,0},{12,4},{16,24},{20,28},{24,16},{28,20},{1,9},{5... | collective-permute-start | bytes 1179656 | tf_op jit(solution)/shard_map/ppermute | solution.py:360
  112.6 1.8 %shard_map.82 = (bf16[256,1024]{1,0:T(8,128)(2,1)}, bf16[256,1024]{1,0:T(8,128)(2,1)}) custom-call(s32[2]{0:T(128)S(1)} %pad_add_fusion.wanted, bf16[256,1024]{1,0:T(8,128)(2,1)S(1)} %copy-done.1, bf16[256,1024]{1,0:T(8,128)(2,1)S(1)} %collective-permute-done.5.refs_1_, bf16[256,1024]{1,0:T(8,128)(2,1)S(1)} %collective-permute-done.6.refs_2_, ...), custom_call_target="tpu_custom_call" | custom-call | tf_op jit(solution)/shard_map/pallas_call | solution.py:273
  114.5 3.7 %collective-permute-done.24.refs_1_ = bf16[128,1536]{1,0:T(8,128)(2,1)S(1)} collective-permute-done((bf16[128,1536]{1,0:T(8,128)(2,1)}, bf16[128,1536]{1,0:T(8,128)(2,1)S(1)}, u32[]{:S(2)}, u32[]{:S(2)}) %collective-permute-start.24) | collective-permute-done | bytes 393248 | tf_op jit(solution)/shard_map/ppermute | solution.py:360
  118.2 2.2 %collective-permute-done.25.refs_3_ = bf16[128,1536]{1,0:T(8,128)(2,1)S(1)} collective-permute-done((bf16[128,1536]{1,0:T(8,128)(2,1)}, bf16[128,1536]{1,0:T(8,128)(2,1)S(1)}, u32[]{:S(2)}, u32[]{:S(2)}) %collective-permute-start.25) | collective-permute-done | bytes 393248 | tf_op jit(solution)/shard_map/ppermute | solution.py:360
  121.3 7.4 %shard_map.87 = (bf16[128,1536]{1,0:T(8,128)(2,1)}, bf16[128,1536]{1,0:T(8,128)(2,1)}, bf16[128,1536]{1,0:T(8,128)(2,1)}, bf16[128,1536]{1,0:T(8,128)(2,1)}) custom-call(s32[1]{0:T(128)} %bitcast.2.core, bf16[3,512,1536]{2,1,0:T(8,128)(2,1)} %own_weight.11, bf16[3,512,1536]{2,1,0:T(8,128)(2,1)} %collective-permute-done.other_weight, ...), custom_call_target="tpu_custom_call" | custom-call | tf_op jit(solution)/shard_map/pallas_call | solution.py:183
  128.7 2.3 %shard_map.89 = (bf16[128,1536]{1,0:T(8,128)(2,1)}, bf16[128,1536]{1,0:T(8,128)(2,1)}) custom-call(bf16[128,1536]{1,0:T(8,128)(2,1)} %get-tuple-element.42.refs_0_, bf16[128,1536]{1,0:T(8,128)(2,1)} %copy-done.16, bf16[128,1536]{1,0:T(8,128)(2,1)} %get-tuple-element.45.refs_2_, bf16[128,1536]{1,0:T(8,128)(2,1)} %copy-done.17), custom_call_target="tpu_custom_call" | custom-call | tf_op jit(solution)/shard_map/pallas_call | solution.py:211
  135.2 12.0 %shard_map.91 = bf16[3,512,1536]{2,1,0:T(8,128)(2,1)} custom-call(s32[1]{0:T(128)} %bitcast.2.core, bf16[256,1024]{1,0:T(8,128)(2,1)} %get-tuple-element.37.refs_0_.refs_1_, bf16[256,1024]{1,0:T(8,128)(2,1)} %collective-permute-done.20.refs_0_.refs_2_.refs_1_, bf16[256,1024]{1,0:T(8,128)(2,1)} %collective-permute-done.21.refs_1_.refs_3_.refs_2_, ...), custom_call_target="tpu_custom_call" | custom-call | tf_op jit(solution)/shard_map/pallas_call | solution.py:321
  147.2 6.2 %shard_map.86 = (bf16[128,1536]{1,0:T(8,128)(2,1)}, bf16[128,1536]{1,0:T(8,128)(2,1)}) custom-call(s32[1]{0:T(128)} %bitcast.2.core, bf16[3,512,1536]{2,1,0:T(8,128)(2,1)} %own_weight.11, bf16[3,512,1536]{2,1,0:T(8,128)(2,1)} %collective-permute-done.other_weight, bf16[256,1024]{1,0:T(8,128)(2,1)} %get-tuple-element.37.refs_0_.refs_1_, ...), custom_call_target="tpu_custom_call" | custom-call | tf_op jit(solution)/shard_map/pallas_call | solution.py:183
  156.3 3.2 %shard_map.90 = (bf16[256,1536]{1,0:T(8,128)(2,1)}, bf16[256,1024]{1,0:T(8,128)(2,1)}) custom-call(f32[8,256]{1,0:T(8,128)} %get-tuple-element.28.places, bf16[256,1024]{1,0:T(8,128)(2,1)S(1)} %copy-done.2, bf16[128,1536]{1,0:T(8,128)(2,1)} %get-tuple-element.38.refs_0_, bf16[128,1536]{1,0:T(8,128)(2,1)} %copy-done.18, ...), custom_call_target="tpu_custom_call" | custom-call | tf_op jit(solution)/shard_map/pallas_call | solution.py:237
  (107 shorter events, 25.7 us)
Async XLA Ops:
  0.6 32.2 %collective-permute-start = (bf16[3,512,1536]{2,1,0:T(8,128)(2,1)}, bf16[3,512,1536]{2,1,0:T(8,128)(2,1)}, u32[]{:S(2)}, u32[]{:S(2)}) collective-permute-start(bf16[3,512,1536]{2,1,0:T(8,128)(2,1)} %own_weight.11), channel_id=1, source_target_pairs={{0,4},{4,0},{8,12},{12,8},{16,20},{20,16},{24,28},{28,24},{1,5},{5... | collective-permute-start | bytes 14155784 | tf_op jit(solution)/shard_map/ppermute | solution.py:363
  4.4 13.2 %collective-permute-start.3 = (bf16[136,1536]{1,0:T(8,128)(2,1)}, bf16[136,1536]{1,0:T(8,128)(2,1)S(1)}, u32[]{:S(2)}, u32[]{:S(2)}) collective-permute-start(bf16[136,1536]{1,0:T(8,128)(2,1)} %get-tuple-element.29.refs_0_.refs_2_.refs_8_.refs_24_), channel_id=1, source_target_pairs={{0,16},{4,20},{8,24},{12,28},{16,0},{20,4},{24,8},{28,12},{1,17},{... | collective-permute-start | bytes 1253384 | tf_op jit(solution)/shard_map/ppermute | solution.py:360
  9.1 15.8 %collective-permute-start.15 = (bf16[256,1024]{1,0:T(8,128)(2,1)}, bf16[256,1024]{1,0:T(8,128)(2,1)S(1)}, u32[]{:S(2)}, u32[]{:S(2)}) collective-permute-start(bf16[256,1024]{1,0:T(8,128)(2,1)} %shard_map.84.refs_0_), channel_id=1, source_target_pairs={{0,1},{1,0},{2,3},{3,2},{4,5},{5,4},{6,7},{7,6},{8,9},{9,8},{10,11... | collective-permute-start | bytes 1572872 | tf_op jit(solution)/shard_map/ppermute | solution.py:375
  10.7 12.7 %collective-permute-start.1 = (bf16[136,1536]{1,0:T(8,128)(2,1)}, bf16[136,1536]{1,0:T(8,128)(2,1)S(1)}, u32[]{:S(2)}, u32[]{:S(2)}) collective-permute-start(bf16[136,1536]{1,0:T(8,128)(2,1)} %get-tuple-element.29.refs_0_.refs_2_.refs_8_.refs_24_), channel_id=1, source_target_pairs={{0,8},{4,12},{8,0},{12,4},{16,24},{20,28},{24,16},{28,20},{1,9},{5... | collective-permute-start | bytes 1253384 | tf_op jit(solution)/shard_map/ppermute | solution.py:360
  12.2 14.4 %collective-permute-start.4 = (bf16[136,1536]{1,0:T(8,128)(2,1)}, bf16[136,1536]{1,0:T(8,128)(2,1)}, u32[]{:S(2)}, u32[]{:S(2)}) collective-permute-start(bf16[136,1536]{1,0:T(8,128)(2,1)} %get-tuple-element.30.refs_1_.refs_3_.refs_9_.refs_25_), channel_id=1, source_target_pairs={{0,16},{4,20},{8,24},{12,28},{16,0},{20,4},{24,8},{28,12},{1,17},{... | collective-permute-start | bytes 1253384 | tf_op jit(solution)/shard_map/ppermute | solution.py:360
  17.6 14.7 %collective-permute-start.2 = (bf16[136,1536]{1,0:T(8,128)(2,1)}, bf16[136,1536]{1,0:T(8,128)(2,1)S(1)}, u32[]{:S(2)}, u32[]{:S(2)}) collective-permute-start(bf16[136,1536]{1,0:T(8,128)(2,1)} %get-tuple-element.30.refs_1_.refs_3_.refs_9_.refs_25_), channel_id=1, source_target_pairs={{0,8},{4,12},{8,0},{12,4},{16,24},{20,28},{24,16},{28,20},{1,9},{5... | collective-permute-start | bytes 1253384 | tf_op jit(solution)/shard_map/ppermute | solution.py:360
  23.4 28.0 %collective-permute-start.16 = (bf16[256,1024]{1,0:T(8,128)(2,1)}, bf16[256,1024]{1,0:T(8,128)(2,1)}, u32[]{:S(2)}, u32[]{:S(2)}) collective-permute-start(bf16[256,1024]{1,0:T(8,128)(2,1)} %shard_map.84.refs_0_), channel_id=1, source_target_pairs={{1,2},{2,1},{5,6},{6,5},{9,10},{10,9},{13,14},{14,13},{17,18},{18,... | collective-permute-start | bytes 1572872 | tf_op jit(solution)/shard_map/ppermute | solution.py:375
  24.9 27.7 %collective-permute-start.18 = (bf16[256,1024]{1,0:T(8,128)(2,1)S(1)}, bf16[256,1024]{1,0:T(8,128)(2,1)}, u32[]{:S(2)}, u32[]{:S(2)}) collective-permute-start(bf16[256,1024]{1,0:T(8,128)(2,1)S(1)} %collective-permute-done.15.refs_1_), channel_id=1, source_target_pairs={{1,2},{2,1},{5,6},{6,5},{9,10},{10,9},{13,14},{14,13},{17,18},{18,... | collective-permute-start | bytes 1572872 | tf_op jit(solution)/shard_map/ppermute | solution.py:375
  26.5 15.8 %collective-permute-start.7 = (bf16[136,1536]{1,0:T(8,128)(2,1)S(1)}, bf16[136,1536]{1,0:T(8,128)(2,1)S(1)}, u32[]{:S(2)}, u32[]{:S(2)}) collective-permute-start(bf16[136,1536]{1,0:T(8,128)(2,1)S(1)} %collective-permute-done.3.refs_2_.refs_5_.refs_12_.refs_28_), channel_id=1, source_target_pairs={{0,8},{4,12},{8,0},{12,4},{16,24},{20,28},{24,16},{28,20},{1,9},{5... | collective-permute-start | bytes 1253384 | tf_op jit(solution)/shard_map/ppermute | solution.py:360
  40.8 13.8 %collective-permute-start.5 = (bf16[256,1024]{1,0:T(8,128)(2,1)}, bf16[256,1024]{1,0:T(8,128)(2,1)S(1)}, u32[]{:S(2)}, u32[]{:S(2)}) collective-permute-start(bf16[256,1024]{1,0:T(8,128)(2,1)} %get-tuple-element.31), channel_id=1, source_target_pairs={{0,8},{4,12},{8,0},{12,4},{16,24},{20,28},{24,16},{28,20},{1,9},{5... | collective-permute-start | bytes 1572872 | tf_op jit(solution)/shard_map/ppermute | solution.py:360
  42.3 23.0 %collective-permute-start.6 = (bf16[256,1024]{1,0:T(8,128)(2,1)}, bf16[256,1024]{1,0:T(8,128)(2,1)S(1)}, u32[]{:S(2)}, u32[]{:S(2)}) collective-permute-start(bf16[256,1024]{1,0:T(8,128)(2,1)} %get-tuple-element.32), channel_id=1, source_target_pairs={{0,16},{4,20},{8,24},{12,28},{16,0},{20,4},{24,8},{28,12},{1,17},{... | collective-permute-start | bytes 1572872 | tf_op jit(solution)/shard_map/ppermute | solution.py:360
  50.6 21.1 %collective-permute-start.9 = (bf16[256,1024]{1,0:T(8,128)(2,1)}, bf16[256,1024]{1,0:T(8,128)(2,1)S(1)}, u32[]{:S(2)}, u32[]{:S(2)}) collective-permute-start(bf16[256,1024]{1,0:T(8,128)(2,1)} %shard_map.79), channel_id=1, source_target_pairs={{0,24},{4,28},{8,16},{12,20},{16,8},{20,12},{24,0},{28,4},{1,25},{... | collective-permute-start | bytes 1572872 | tf_op jit(solution)/shard_map/ppermute | solution.py:360
  51.4 25.1 %collective-permute-start.17 = (bf16[256,1024]{1,0:T(8,128)(2,1)}, bf16[256,1024]{1,0:T(8,128)(2,1)}, u32[]{:S(2)}, u32[]{:S(2)}) collective-permute-start(bf16[256,1024]{1,0:T(8,128)(2,1)} %collective-permute-done.16.refs_2_), channel_id=1, source_target_pairs={{1,0},{2,3},{5,4},{6,7},{9,8},{10,11},{13,12},{14,15},{17,16},{18,... | collective-permute-start | bytes 1572872 | tf_op jit(solution)/shard_map/ppermute | solution.py:375
  52.7 24.1 %collective-permute-start.19 = (bf16[256,1024]{1,0:T(8,128)(2,1)}, bf16[256,1024]{1,0:T(8,128)(2,1)}, u32[]{:S(2)}, u32[]{:S(2)}) collective-permute-start(bf16[256,1024]{1,0:T(8,128)(2,1)} %collective-permute-done.18.refs_4_), channel_id=1, source_target_pairs={{1,0},{2,3},{5,4},{6,7},{9,8},{10,11},{13,12},{14,15},{17,16},{18,... | collective-permute-start | bytes 1572872 | tf_op jit(solution)/shard_map/ppermute | solution.py:375
  54.6 21.5 %collective-permute-start.33 = (bf16[136,1536]{1,0:T(8,128)(2,1)}, bf16[136,1536]{1,0:T(8,128)(2,1)}, u32[]{:S(2)}, u32[]{:S(2)}) collective-permute-start(bf16[136,1536]{1,0:T(8,128)(2,1)} %get-tuple-element.29.refs_0_.refs_2_.refs_8_.refs_24_), channel_id=1, source_target_pairs={{0,4},{4,0},{8,12},{12,8},{16,20},{20,16},{24,28},{28,24},{1,5},{5... | collective-permute-start | bytes 1253384 | tf_op jit(solution)/shard_map/ppermute | solution.py:363
  65.3 15.1 %collective-permute-start.34 = (bf16[136,1536]{1,0:T(8,128)(2,1)}, bf16[136,1536]{1,0:T(8,128)(2,1)}, u32[]{:S(2)}, u32[]{:S(2)}) collective-permute-start(bf16[136,1536]{1,0:T(8,128)(2,1)} %get-tuple-element.30.refs_1_.refs_3_.refs_9_.refs_25_), channel_id=1, source_target_pairs={{0,4},{4,0},{8,12},{12,8},{16,20},{20,16},{24,28},{28,24},{1,5},{5... | collective-permute-start | bytes 1253384 | tf_op jit(solution)/shard_map/ppermute | solution.py:363
  73.6 14.6 %collective-permute-start.10 = (bf16[256,1024]{1,0:T(8,128)(2,1)}, bf16[256,1024]{1,0:T(8,128)(2,1)S(1)}, u32[]{:S(2)}, u32[]{:S(2)}) collective-permute-start(bf16[256,1024]{1,0:T(8,128)(2,1)} %shard_map.80), channel_id=1, source_target_pairs={{0,1},{3,2},{4,5},{7,6},{8,9},{11,10},{12,13},{15,14},{16,17},{19,... | collective-permute-start | bytes 1572872 | tf_op jit(solution)/shard_map/ppermute | solution.py:375
  80.5 19.6 %collective-permute-start.23 = (bf16[256,1024]{1,0:T(8,128)(2,1)}, bf16[256,1024]{1,0:T(8,128)(2,1)}, u32[]{:S(2)}, u32[]{:S(2)}) collective-permute-start(bf16[256,1024]{1,0:T(8,128)(2,1)} %get-tuple-element.43), channel_id=1, source_target_pairs={{0,24},{4,28},{8,16},{12,20},{16,8},{20,12},{24,0},{28,4},{1,25},{... | collective-permute-start | bytes 1572872 | tf_op jit(solution)/shard_map/ppermute | solution.py:360
  88.2 18.5 %collective-permute-start.20 = (bf16[256,1024]{1,0:T(8,128)(2,1)}, bf16[256,1024]{1,0:T(8,128)(2,1)}, u32[]{:S(2)}, u32[]{:S(2)}) collective-permute-start(bf16[256,1024]{1,0:T(8,128)(2,1)} %get-tuple-element.39), channel_id=1, source_target_pairs={{0,8},{4,12},{8,0},{12,4},{16,24},{20,28},{24,16},{28,20},{1,9},{5... | collective-permute-start | bytes 1572872 | tf_op jit(solution)/shard_map/ppermute | solution.py:360
  90.1 17.8 %collective-permute-start.21 = (bf16[256,1024]{1,0:T(8,128)(2,1)}, bf16[256,1024]{1,0:T(8,128)(2,1)}, u32[]{:S(2)}, u32[]{:S(2)}) collective-permute-start(bf16[256,1024]{1,0:T(8,128)(2,1)} %get-tuple-element.40), channel_id=1, source_target_pairs={{0,16},{4,20},{8,24},{12,28},{16,0},{20,4},{24,8},{28,12},{1,17},{... | collective-permute-start | bytes 1572872 | tf_op jit(solution)/shard_map/ppermute | solution.py:360
  91.1 16.7 %collective-permute-start.11 = (bf16[256,1024]{1,0:T(8,128)(2,1)}, bf16[256,1024]{1,0:T(8,128)(2,1)S(1)}, u32[]{:S(2)}, u32[]{:S(2)}) collective-permute-start(bf16[256,1024]{1,0:T(8,128)(2,1)} %get-tuple-element.33), channel_id=1, source_target_pairs={{2,1},{1,2},{6,5},{5,6},{10,9},{9,10},{14,13},{13,14},{18,17},{17,... | collective-permute-start | bytes 1572872 | tf_op jit(solution)/shard_map/ppermute | solution.py:375
  91.9 19.0 %collective-permute-start.12 = (bf16[256,1024]{1,0:T(8,128)(2,1)}, bf16[256,1024]{1,0:T(8,128)(2,1)S(1)}, u32[]{:S(2)}, u32[]{:S(2)}) collective-permute-start(bf16[256,1024]{1,0:T(8,128)(2,1)} %get-tuple-element.34), channel_id=1, source_target_pairs={{0,1},{3,2},{4,5},{7,6},{8,9},{11,10},{12,13},{15,14},{16,17},{19,... | collective-permute-start | bytes 1572872 | tf_op jit(solution)/shard_map/ppermute | solution.py:375
  100.1 14.3 %collective-permute-start.29 = (bf16[256,1024]{1,0:T(8,128)(2,1)}, bf16[256,1024]{1,0:T(8,128)(2,1)}, u32[]{:S(2)}, u32[]{:S(2)}) collective-permute-start(bf16[256,1024]{1,0:T(8,128)(2,1)} %get-tuple-element.37.refs_0_.refs_1_), channel_id=1, source_target_pairs={{0,4},{4,0},{8,12},{12,8},{16,20},{20,16},{24,28},{28,24},{1,5},{5... | collective-permute-start | bytes 1572872 | tf_op jit(solution)/shard_map/ppermute | solution.py:363
  107.8 23.2 %collective-permute-start.30 = (bf16[256,1024]{1,0:T(8,128)(2,1)}, bf16[256,1024]{1,0:T(8,128)(2,1)S(1)}, u32[]{:S(2)}, u32[]{:S(2)}) collective-permute-start(bf16[256,1024]{1,0:T(8,128)(2,1)} %collective-permute-done.20.refs_0_.refs_2_.refs_1_), channel_id=1, source_target_pairs={{0,4},{4,0},{8,12},{12,8},{16,20},{20,16},{24,28},{28,24},{1,5},{5... | collective-permute-start | bytes 1572872 | tf_op jit(solution)/shard_map/ppermute | solution.py:363
  107.8 24.7 %collective-permute-start.31 = (bf16[256,1024]{1,0:T(8,128)(2,1)}, bf16[256,1024]{1,0:T(8,128)(2,1)S(1)}, u32[]{:S(2)}, u32[]{:S(2)}) collective-permute-start(bf16[256,1024]{1,0:T(8,128)(2,1)} %collective-permute-done.21.refs_1_.refs_3_.refs_2_), channel_id=1, source_target_pairs={{0,4},{4,0},{8,12},{12,8},{16,20},{20,16},{24,28},{28,24},{1,5},{5... | collective-permute-start | bytes 1572872 | tf_op jit(solution)/shard_map/ppermute | solution.py:363
  114.4 19.1 %collective-permute-start.32 = (bf16[256,1024]{1,0:T(8,128)(2,1)}, bf16[256,1024]{1,0:T(8,128)(2,1)S(1)}, u32[]{:S(2)}, u32[]{:S(2)}) collective-permute-start(bf16[256,1024]{1,0:T(8,128)(2,1)} %collective-permute-done.23.refs_0_.refs_1_.refs_3_), channel_id=1, source_target_pairs={{0,4},{4,0},{8,12},{12,8},{16,20},{20,16},{24,28},{28,24},{1,5},{5... | collective-permute-start | bytes 1572872 | tf_op jit(solution)/shard_map/ppermute | solution.py:363
  118.2 16.4 %collective-permute-start.13 = (bf16[256,1024]{1,0:T(8,128)(2,1)}, bf16[256,1024]{1,0:T(8,128)(2,1)S(1)}, u32[]{:S(2)}, u32[]{:S(2)}) collective-permute-start(bf16[256,1024]{1,0:T(8,128)(2,1)} %get-tuple-element.35), channel_id=1, source_target_pairs={{1,0},{0,1},{3,2},{2,3},{5,4},{4,5},{7,6},{6,7},{9,8},{8,9},{11,10... | collective-permute-start | bytes 1572872 | tf_op jit(solution)/shard_map/ppermute | solution.py:375
  120.4 33.0 %collective-permute-start.14 = (bf16[256,1024]{1,0:T(8,128)(2,1)}, bf16[256,1024]{1,0:T(8,128)(2,1)S(1)}, u32[]{:S(2)}, u32[]{:S(2)}) collective-permute-start(bf16[256,1024]{1,0:T(8,128)(2,1)} %get-tuple-element.36), channel_id=1, source_target_pairs={{2,1},{1,2},{6,5},{5,6},{10,9},{9,10},{14,13},{13,14},{18,17},{17,... | collective-permute-start | bytes 1572872 | tf_op jit(solution)/shard_map/ppermute | solution.py:375
  131.0 23.5 %collective-permute-start.22 = (bf16[128,1536]{1,0:T(8,128)(2,1)}, bf16[128,1536]{1,0:T(8,128)(2,1)S(1)}, u32[]{:S(2)}, u32[]{:S(2)}) collective-permute-start(bf16[128,1536]{1,0:T(8,128)(2,1)} %get-tuple-element.41), channel_id=1, source_target_pairs={{0,8},{4,12},{8,0},{12,4},{16,24},{20,28},{24,16},{28,20},{1,9},{5... | collective-permute-start | bytes 1179656 | tf_op jit(solution)/shard_map/ppermute | solution.py:360
  132.5 22.0 %collective-permute-start.28 = (bf16[128,1536]{1,0:T(8,128)(2,1)}, bf16[128,1536]{1,0:T(8,128)(2,1)}, u32[]{:S(2)}, u32[]{:S(2)}) collective-permute-start(bf16[128,1536]{1,0:T(8,128)(2,1)} %get-tuple-element.50), channel_id=1, source_target_pairs={{0,16},{4,20},{8,24},{12,28},{16,0},{20,4},{24,8},{28,12},{1,17},{... | collective-permute-start | bytes 1179656 | tf_op jit(solution)/shard_map/ppermute | solution.py:360
  133.5 21.0 %collective-permute-start.26 = (bf16[128,1536]{1,0:T(8,128)(2,1)}, bf16[128,1536]{1,0:T(8,128)(2,1)}, u32[]{:S(2)}, u32[]{:S(2)}) collective-permute-start(bf16[128,1536]{1,0:T(8,128)(2,1)} %get-tuple-element.47), channel_id=1, source_target_pairs={{0,16},{4,20},{8,24},{12,28},{16,0},{20,4},{24,8},{28,12},{1,17},{... | collective-permute-start | bytes 1179656 | tf_op jit(solution)/shard_map/ppermute | solution.py:360
  134.6 20.0 %collective-permute-start.27 = (bf16[128,1536]{1,0:T(8,128)(2,1)}, bf16[128,1536]{1,0:T(8,128)(2,1)}, u32[]{:S(2)}, u32[]{:S(2)}) collective-permute-start(bf16[128,1536]{1,0:T(8,128)(2,1)} %get-tuple-element.49), channel_id=1, source_target_pairs={{0,8},{4,12},{8,0},{12,4},{16,24},{20,28},{24,16},{28,20},{1,9},{5... | collective-permute-start | bytes 1179656 | tf_op jit(solution)/shard_map/ppermute | solution.py:360
  (28 other events, 212.0 us)

commit v2 on v1

--- a/solution.py
+++ b/solution.py
@@ -146,7 +146,7 @@
         ),
         out_shape=[pltpu.HBM((size, 2 * half), BF16) for size in sizes],
         compiler_params=limit(28),
-    )(core, *in_hbm(own_weight, other_weight, *blocks))
+    )(core, *in_hbm(own_weight, other_weight), *blocks)
 
 
 def project_kernel(core, own_weight, other_weight, *refs, items):
@@ -192,7 +192,7 @@
         ),
         out_shape=[pltpu.HBM((cut, columns), BF16)] * len(items),
         compiler_params=limit(28),
-    )(core, *in_hbm(own_weight, other_weight, *[item[0] for item in items], *[item[2] for item in items]))
+    )(core, *in_hbm(own_weight, other_weight), *[item[0] for item in items], *in_hbm(*[item[2] for item in items]))
 
 
 def total_kernel(*refs, counts):
@@ -241,7 +241,7 @@
         out_specs=[whole(shape) for shape in shapes],
         out_shape=[jax.ShapeDtypeStruct(shape, BF16) for shape in shapes],
         compiler_params=limit(20),
-    )(*in_hbm(places), term, *in_hbm(*first, *second))
+    )(*in_hbm(places, term), *first, *second)
 
 
 def fold_kernel(wanted, *refs, sources, counts):
@@ -404,10 +404,13 @@
 
     arrived = {}
     for group in ([0], bits, several):
-        made = input_terms(core, halves_of(group), [row_count] * len(group), qkv_weight, other_weight)
+        blocks = halves_of(group)
+        made = input_terms(
+            core, blocks if group == several else in_hbm(*blocks), [row_count] * len(group), qkv_weight, other_weight
+        )
         for offset, term in zip(group, made):
             arrived[offset] = across(term, offset) if offset else term
-    all_terms = [arrived[offset] for offset in range(chip_count)]
+    all_terms = in_hbm(*[arrived[offset] for offset in range(chip_count)])
 
     def term_number(where):
         return chip ^ jnp.clip(where, 0, tp_count - 1)

time: 161 us -> 163 us (1.012)
  Pallas kernels: 71.9 us -> 75.1 us
    pallas_call x5, Pallas kernels: 8.86 us -> 12.8 us  [fold(): pl.pallas_call(functools.partial(fold_kernel, sources=len(sources), count...]
    unnamed x38 -> x44, local copies, waits for them, and re-layouts: 3.92 us -> 3.11 us
  transfers between devices with their start and end apart: 41 -> 41, of which waited for: 11 -> 10; matrix products, arithmetic and copies ran while one was open for 0% -> 0% of each run, Pallas kernels for 43% -> 45%
where the time goes in v2:
time: 163 us; the launch traced here: 161 us
  Pallas kernels  75.1 us (46%)
  starting transfers between devices  42.6 us (26%)
  waiting for transfers between devices  39.1 us (24%)
  local copies, waits for them, and re-layouts  3.11 us (2%)
    ppermute x18, waiting for transfers between devices, across(): return lax.ppermute(value, 'loop', pairs)  29.9 us
    pallas_call x3, Pallas kernels, input_terms(): pl.pallas_call(functools.partial(input_kernel, blocks=len(blocks), tile=t...  20.3 us
    ppermute x18, starting transfers between devices, across(): return lax.ppermute(value, 'loop', pairs)  20.3 us
    pallas_call x3, Pallas kernels, project_parts(): pl.pallas_call(functools.partial(project_kernel, items=len(items)), grid_...  19.5 us
    ppermute x10, starting transfers between devices, along(): return lax.ppermute(value, 'tp', pairs)  19.3 us
    pallas_call x5, Pallas kernels, fold(): pl.pallas_call(functools.partial(fold_kernel, sources=len(sources), count...  12.8 us
    pallas_call x1, Pallas kernels, weight_gradient(): pl.pallas_call(functools.partial(weight_kernel, blocks=len(blocks), grads...  12 us
    ppermute x10, waiting for transfers between devices, along(): return lax.ppermute(value, 'tp', pairs)  9.07 us
  transfers between devices with their start and end apart: 41, of which 10 were waited for; matrix products, arithmetic and copies ran while one was open for 0% of the time, Pallas kernels for 45%

profile of v2, /device:TPU:0, one launch (start us, length us, event | category | flops | bytes accessed | tf_op | source)
XLA Modules:
  0.0 161.2 jit_solution(3505308455797729727)
XLA Ops:
  1.2 3.2 %shard_map.76 = (bf16[136,1536]{1,0:T(8,128)(2,1)}, bf16[136,1536]{1,0:T(8,128)(2,1)}, f32[8,256]{1,0:T(8,128)}) custom-call(s32[8]{0:T(128)} %kinds_of_loops.1, s32[1,256]{1,0:T(1,128)} %bitcast.12, bf16[256,1536]{1,0:T(8,128)(2,1)} %grads.1), custom_call_target="tpu_custom_call" | custom-call | tf_op jit(solution)/shard_map/pallas_call | solution.py:61
  4.4 2.5 %collective-permute-start.3 = (bf16[136,1536]{1,0:T(8,128)(2,1)}, bf16[136,1536]{1,0:T(8,128)(2,1)S(1)}, u32[]{:S(2)}, u32[]{:S(2)}) collective-permute-start(bf16[136,1536]{1,0:T(8,128)(2,1)} %get-tuple-element.29.refs_0_.refs_2_.refs_8_.refs_24_), channel_id=1, source_target_pairs={{0,16},{4,20},{8,24},{12,28},{16,0},{20,4},{24,8},{28,12},{1,17},{... | collective-permute-start | bytes 1253384 | tf_op jit(solution)/shard_map/ppermute | solution.py:360
  6.9 2.2 %shard_map.84.refs_0_ = bf16[256,1024]{1,0:T(8,128)(2,1)} custom-call(f32[8,256]{1,0:T(8,128)} %get-tuple-element.28.places, bf16[256,1024]{1,0:T(8,128)(2,1)} %rows.1), custom_call_target="tpu_custom_call" | custom-call | tf_op jit(solution)/shard_map/pallas_call | solution.py:81
  12.7 5.0 %collective-permute-done.3.refs_2_.refs_5_.refs_12_.refs_28_ = bf16[136,1536]{1,0:T(8,128)(2,1)S(1)} collective-permute-done((bf16[136,1536]{1,0:T(8,128)(2,1)}, bf16[136,1536]{1,0:T(8,128)(2,1)S(1)}, u32[]{:S(2)}, u32[]{:S(2)}) %collective-permute-start.3) | collective-permute-done | bytes 417824 | tf_op jit(solution)/shard_map/ppermute | solution.py:360
  17.6 2.0 %collective-permute-start.2 = (bf16[136,1536]{1,0:T(8,128)(2,1)}, bf16[136,1536]{1,0:T(8,128)(2,1)S(1)}, u32[]{:S(2)}, u32[]{:S(2)}) collective-permute-start(bf16[136,1536]{1,0:T(8,128)(2,1)} %get-tuple-element.30.refs_1_.refs_3_.refs_9_.refs_25_), channel_id=1, source_target_pairs={{0,8},{4,12},{8,0},{12,4},{16,24},{20,28},{24,16},{28,20},{1,9},{5... | collective-permute-start | bytes 1253384 | tf_op jit(solution)/shard_map/ppermute | solution.py:360
  19.6 3.9 %collective-permute-done.1.refs_0_.refs_4_.refs_10_.refs_26_ = bf16[136,1536]{1,0:T(8,128)(2,1)} collective-permute-done((bf16[136,1536]{1,0:T(8,128)(2,1)}, bf16[136,1536]{1,0:T(8,128)(2,1)}, u32[]{:S(2)}, u32[]{:S(2)}) %collective-permute-start.1) | collective-permute-done | bytes 417824 | tf_op jit(solution)/shard_map/ppermute | solution.py:360
  26.5 1.7 %collective-permute-start.7 = (bf16[136,1536]{1,0:T(8,128)(2,1)S(1)}, bf16[136,1536]{1,0:T(8,128)(2,1)S(1)}, u32[]{:S(2)}, u32[]{:S(2)}) collective-permute-start(bf16[136,1536]{1,0:T(8,128)(2,1)S(1)} %collective-permute-done.3.refs_2_.refs_5_.refs_12_.refs_28_), channel_id=1, source_target_pairs={{0,8},{4,12},{8,0},{12,4},{16,24},{20,28},{24,16},{28,20},{1,9},{5... | collective-permute-start | bytes 1253384 | tf_op jit(solution)/shard_map/ppermute | solution.py:360
  28.2 4.1 %collective-permute-done.2.refs_1_.refs_6_.refs_11_.refs_27_ = bf16[136,1536]{1,0:T(8,128)(2,1)S(1)} collective-permute-done((bf16[136,1536]{1,0:T(8,128)(2,1)}, bf16[136,1536]{1,0:T(8,128)(2,1)S(1)}, u32[]{:S(2)}, u32[]{:S(2)}) %collective-permute-start.2) | collective-permute-done | bytes 417824 | tf_op jit(solution)/shard_map/ppermute | solution.py:360
  33.2 7.6 %shard_map.78 = (bf16[256,1024]{1,0:T(8,128)(2,1)}, bf16[256,1024]{1,0:T(8,128)(2,1)}) custom-call(s32[1]{0:T(128)} %bitcast.2.core, bf16[3,512,1536]{2,1,0:T(8,128)(2,1)} %own_weight.11, bf16[3,512,1536]{2,1,0:T(8,128)(2,1)} %collective-permute-done.other_weight, bf16[136,1536]{1,0:T(8,128)(2,1)} %collective-permute-done.1.refs_0_.refs_4_.refs_10_.refs_26_, ...), custom_call_target="tpu_custom_call" | custom-call | tf_op jit(solution)/shard_map/pallas_call | solution.py:139
  43.6 6.2 %shard_map.79 = bf16[256,1024]{1,0:T(8,128)(2,1)} custom-call(s32[1]{0:T(128)} %bitcast.2.core, bf16[3,512,1536]{2,1,0:T(8,128)(2,1)} %own_weight.11, bf16[3,512,1536]{2,1,0:T(8,128)(2,1)} %collective-permute-done.other_weight, bf16[136,1536]{1,0:T(8,128)(2,1)S(1)} %collective-permute-done.7.refs_0_.refs_2_.refs_14_.refs_30_, ...), custom_call_target="tpu_custom_call" | custom-call | tf_op jit(solution)/shard_map/pallas_call | solution.py:139
  53.1 2.3 %collective-permute-done.5.refs_1_ = bf16[256,1024]{1,0:T(8,128)(2,1)S(1)} collective-permute-done((bf16[256,1024]{1,0:T(8,128)(2,1)}, bf16[256,1024]{1,0:T(8,128)(2,1)S(1)}, u32[]{:S(2)}, u32[]{:S(2)}) %collective-permute-start.5) | collective-permute-done | bytes 524320 | tf_op jit(solution)/shard_map/ppermute | solution.py:360
  55.5 9.9 %collective-permute-done.6.refs_2_ = bf16[256,1024]{1,0:T(8,128)(2,1)S(1)} collective-permute-done((bf16[256,1024]{1,0:T(8,128)(2,1)}, bf16[256,1024]{1,0:T(8,128)(2,1)S(1)}, u32[]{:S(2)}, u32[]{:S(2)}) %collective-permute-start.6) | collective-permute-done | bytes 524320 | tf_op jit(solution)/shard_map/ppermute | solution.py:360
  65.3 6.5 %shard_map.77.refs_0_ = bf16[256,1024]{1,0:T(8,128)(2,1)} custom-call(s32[1]{0:T(128)} %bitcast.2.core, bf16[3,512,1536]{2,1,0:T(8,128)(2,1)} %own_weight.11, bf16[3,512,1536]{2,1,0:T(8,128)(2,1)} %collective-permute-done.other_weight, bf16[136,1536]{1,0:T(8,128)(2,1)} %get-tuple-element.29.refs_0_.refs_2_.refs_8_.refs_24_, ...), custom_call_target="tpu_custom_call" | custom-call | tf_op jit(solution)/shard_map/pallas_call | solution.py:139
  72.6 1.9 %shard_map.80 = bf16[256,1024]{1,0:T(8,128)(2,1)} custom-call(s32[1]{0:T(128)} %bitcast.7.wanted, bf16[256,1024]{1,0:T(8,128)(2,1)} %shard_map.77.refs_0_, bf16[256,1024]{1,0:T(8,128)(2,1)} %copy-done.8, bf16[256,1024]{1,0:T(8,128)(2,1)} %copy-done.9, bf16[256,1024]{1,0:T(8,128)(2,1)} %copy-done.10), custom_call_target="tpu_custom_call" | custom-call | tf_op jit(solution)/shard_map/pallas_call | solution.py:273
  74.5 2.5 %collective-permute-start.10 = (bf16[256,1024]{1,0:T(8,128)(2,1)}, bf16[256,1024]{1,0:T(8,128)(2,1)S(1)}, u32[]{:S(2)}, u32[]{:S(2)}) collective-permute-start(bf16[256,1024]{1,0:T(8,128)(2,1)} %shard_map.80), channel_id=1, source_target_pairs={{0,1},{3,2},{4,5},{7,6},{8,9},{11,10},{12,13},{15,14},{16,17},{19,... | collective-permute-start | bytes 1572872 | tf_op jit(solution)/shard_map/ppermute | solution.py:375
  77.8 3.4 %shard_map.85 = (bf16[256,1024]{1,0:T(8,128)(2,1)}, bf16[256,1024]{1,0:T(8,128)(2,1)}, bf16[256,1024]{1,0:T(8,128)(2,1)}, bf16[256,1024]{1,0:T(8,128)(2,1)}) custom-call(s32[4]{0:T(128)S(1)} %pad_add_fusion.2.wanted, bf16[256,1024]{1,0:T(8,128)(2,1)} %shard_map.84.refs_0_, bf16[256,1024]{1,0:T(8,128)(2,1)} %collective-permute-done.15.refs_1_, ...), custom_call_target="tpu_custom_call" | custom-call | tf_op jit(solution)/shard_map/pallas_call | solution.py:273
  82.4 6.5 %collective-permute-done.10.refs_4_ = bf16[256,1024]{1,0:T(8,128)(2,1)S(1)} collective-permute-done((bf16[256,1024]{1,0:T(8,128)(2,1)}, bf16[256,1024]{1,0:T(8,128)(2,1)S(1)}, u32[]{:S(2)}, u32[]{:S(2)}) %collective-permute-start.10) | collective-permute-done | bytes 524320 | tf_op jit(solution)/shard_map/ppermute | solution.py:375
  89.0 2.7 %shard_map.81 = (bf16[256,1024]{1,0:T(8,128)(2,1)}, bf16[256,1024]{1,0:T(8,128)(2,1)}) custom-call(s32[2]{0:T(128)S(1)} %pad_add_fusion.1.wanted, bf16[256,1024]{1,0:T(8,128)(2,1)} %shard_map.77.refs_0_, bf16[256,1024]{1,0:T(8,128)(2,1)} %copy-done.8, bf16[256,1024]{1,0:T(8,128)(2,1)} %copy-done.9, bf16[256,1024]{1,0:T(8,128)(2,1)} %copy-done.10, ...), custom_call_target="tpu_custom_call" | custom-call | tf_op jit(solution)/shard_map/pallas_call | solution.py:273
  93.6 8.2 %collective-permute-start.12 = (bf16[256,1024]{1,0:T(8,128)(2,1)}, bf16[256,1024]{1,0:T(8,128)(2,1)S(1)}, u32[]{:S(2)}, u32[]{:S(2)}) collective-permute-start(bf16[256,1024]{1,0:T(8,128)(2,1)} %get-tuple-element.34), channel_id=1, source_target_pairs={{0,1},{3,2},{4,5},{7,6},{8,9},{11,10},{12,13},{15,14},{16,17},{19,... | collective-permute-start | bytes 1572872 | tf_op jit(solution)/shard_map/ppermute | solution.py:375
  101.9 6.2 %shard_map.88 = (bf16[128,1536]{1,0:T(8,128)(2,1)}, bf16[128,1536]{1,0:T(8,128)(2,1)}) custom-call(s32[1]{0:T(128)} %bitcast.2.core, bf16[3,512,1536]{2,1,0:T(8,128)(2,1)} %own_weight.11, bf16[3,512,1536]{2,1,0:T(8,128)(2,1)} %collective-permute-done.other_weight, bf16[256,1024]{1,0:T(8,128)(2,1)S(1)} %collective-permute-done.23.refs_0_.refs_1_.refs_3_, ...), custom_call_target="tpu_custom_call" | custom-call | tf_op jit(solution)/shard_map/pallas_call | solution.py:183
  109.8 2.5 %collective-permute-done.12.refs_5_ = bf16[256,1024]{1,0:T(8,128)(2,1)S(1)} collective-permute-done((bf16[256,1024]{1,0:T(8,128)(2,1)}, bf16[256,1024]{1,0:T(8,128)(2,1)S(1)}, u32[]{:S(2)}, u32[]{:S(2)}) %collective-permute-start.12) | collective-permute-done | bytes 524320 | tf_op jit(solution)/shard_map/ppermute | solution.py:375
  112.3 1.7 %collective-permute-start.25 = (bf16[128,1536]{1,0:T(8,128)(2,1)}, bf16[128,1536]{1,0:T(8,128)(2,1)S(1)}, u32[]{:S(2)}, u32[]{:S(2)}) collective-permute-start(bf16[128,1536]{1,0:T(8,128)(2,1)} %get-tuple-element.46), channel_id=1, source_target_pairs={{0,8},{4,12},{8,0},{12,4},{16,24},{20,28},{24,16},{28,20},{1,9},{5... | collective-permute-start | bytes 1179656 | tf_op jit(solution)/shard_map/ppermute | solution.py:360
  114.1 2.7 %shard_map.82 = (bf16[256,1024]{1,0:T(8,128)(2,1)}, bf16[256,1024]{1,0:T(8,128)(2,1)}) custom-call(s32[2]{0:T(128)S(1)} %pad_add_fusion.wanted, bf16[256,1024]{1,0:T(8,128)(2,1)} %shard_map.77.refs_0_, bf16[256,1024]{1,0:T(8,128)(2,1)} %copy-done.8, bf16[256,1024]{1,0:T(8,128)(2,1)} %copy-done.9, bf16[256,1024]{1,0:T(8,128)(2,1)} %copy-done.10, ...), custom_call_target="tpu_custom_call" | custom-call | tf_op jit(solution)/shard_map/pallas_call | solution.py:273
  116.9 2.9 %collective-permute-done.24.refs_1_ = bf16[128,1536]{1,0:T(8,128)(2,1)S(1)} collective-permute-done((bf16[128,1536]{1,0:T(8,128)(2,1)}, bf16[128,1536]{1,0:T(8,128)(2,1)S(1)}, u32[]{:S(2)}, u32[]{:S(2)}) %collective-permute-start.24) | collective-permute-done | bytes 393248 | tf_op jit(solution)/shard_map/ppermute | solution.py:360
  119.8 1.8 %collective-permute-done.25.refs_3_ = bf16[128,1536]{1,0:T(8,128)(2,1)S(1)} collective-permute-done((bf16[128,1536]{1,0:T(8,128)(2,1)}, bf16[128,1536]{1,0:T(8,128)(2,1)S(1)}, u32[]{:S(2)}, u32[]{:S(2)}) %collective-permute-start.25) | collective-permute-done | bytes 393248 | tf_op jit(solution)/shard_map/ppermute | solution.py:360
  122.5 7.2 %shard_map.87 = (bf16[128,1536]{1,0:T(8,128)(2,1)}, bf16[128,1536]{1,0:T(8,128)(2,1)}, bf16[128,1536]{1,0:T(8,128)(2,1)}, bf16[128,1536]{1,0:T(8,128)(2,1)}) custom-call(s32[1]{0:T(128)} %bitcast.2.core, bf16[3,512,1536]{2,1,0:T(8,128)(2,1)} %own_weight.11, bf16[3,512,1536]{2,1,0:T(8,128)(2,1)} %collective-permute-done.other_weight, ...), custom_call_target="tpu_custom_call" | custom-call | tf_op jit(solution)/shard_map/pallas_call | solution.py:183
  129.7 2.3 %shard_map.89 = (bf16[128,1536]{1,0:T(8,128)(2,1)}, bf16[128,1536]{1,0:T(8,128)(2,1)}) custom-call(bf16[128,1536]{1,0:T(8,128)(2,1)} %get-tuple-element.42.refs_0_, bf16[128,1536]{1,0:T(8,128)(2,1)} %copy-done.20, bf16[128,1536]{1,0:T(8,128)(2,1)} %get-tuple-element.45.refs_2_, bf16[128,1536]{1,0:T(8,128)(2,1)} %copy-done.21), custom_call_target="tpu_custom_call" | custom-call | tf_op jit(solution)/shard_map/pallas_call | solution.py:211
  132.0 1.6 collective-permute-start.22
  136.2 12.0 %shard_map.91 = bf16[3,512,1536]{2,1,0:T(8,128)(2,1)} custom-call(s32[1]{0:T(128)} %bitcast.2.core, bf16[256,1024]{1,0:T(8,128)(2,1)} %get-tuple-element.37.refs_0_.refs_1_, bf16[256,1024]{1,0:T(8,128)(2,1)} %copy-done.4, bf16[256,1024]{1,0:T(8,128)(2,1)} %copy-done.5, bf16[256,1024]{1,0:T(8,128)(2,1)} %copy-done.3, ...), custom_call_target="tpu_custom_call" | custom-call | tf_op jit(solution)/shard_map/pallas_call | solution.py:321
  148.3 6.1 %shard_map.86 = (bf16[128,1536]{1,0:T(8,128)(2,1)}, bf16[128,1536]{1,0:T(8,128)(2,1)}) custom-call(s32[1]{0:T(128)} %bitcast.2.core, bf16[3,512,1536]{2,1,0:T(8,128)(2,1)} %own_weight.11, bf16[3,512,1536]{2,1,0:T(8,128)(2,1)} %collective-permute-done.other_weight, bf16[256,1024]{1,0:T(8,128)(2,1)S(1)} %copy-done.2, bf16[256,1024]{1,0:T(8,128)(2,1)S(1)} %copy-done.2, ...), custom_call_target="tpu_custom_call" | custom-call | tf_op jit(solution)/shard_map/pallas_call | solution.py:183
  154.4 2.0 %shard_map.83.term = bf16[256,1024]{1,0:T(8,128)(2,1)} custom-call(s32[1]{0:T(128)} %bitcast.1.wanted, bf16[256,1024]{1,0:T(8,128)(2,1)} %shard_map.77.refs_0_, bf16[256,1024]{1,0:T(8,128)(2,1)} %copy-done.8, bf16[256,1024]{1,0:T(8,128)(2,1)} %copy-done.9, bf16[256,1024]{1,0:T(8,128)(2,1)} %copy-done.10, ...), custom_call_target="tpu_custom_call" | custom-call | tf_op jit(solution)/shard_map/pallas_call | solution.py:273
  158.5 2.7 %shard_map.90 = (bf16[256,1536]{1,0:T(8,128)(2,1)}, bf16[256,1024]{1,0:T(8,128)(2,1)}) custom-call(f32[8,256]{1,0:T(8,128)} %get-tuple-element.28.places, bf16[256,1024]{1,0:T(8,128)(2,1)} %shard_map.83.term, bf16[128,1536]{1,0:T(8,128)(2,1)S(1)} %copy-done.6, bf16[128,1536]{1,0:T(8,128)(2,1)S(1)} %collective-permute-done.22.refs_1_, ...), custom_call_target="tpu_custom_call" | custom-call | tf_op jit(solution)/shard_map/pallas_call | solution.py:237
  (113 shorter events, 25.8 us)
Async XLA Ops:
  0.6 32.2 %collective-permute-start = (bf16[3,512,1536]{2,1,0:T(8,128)(2,1)}, bf16[3,512,1536]{2,1,0:T(8,128)(2,1)}, u32[]{:S(2)}, u32[]{:S(2)}) collective-permute-start(bf16[3,512,1536]{2,1,0:T(8,128)(2,1)} %own_weight.11), channel_id=1, source_target_pairs={{0,4},{4,0},{8,12},{12,8},{16,20},{20,16},{24,28},{28,24},{1,5},{5... | collective-permute-start | bytes 14155784 | tf_op jit(solution)/shard_map/ppermute | solution.py:363
  4.4 13.2 %collective-permute-start.3 = (bf16[136,1536]{1,0:T(8,128)(2,1)}, bf16[136,1536]{1,0:T(8,128)(2,1)S(1)}, u32[]{:S(2)}, u32[]{:S(2)}) collective-permute-start(bf16[136,1536]{1,0:T(8,128)(2,1)} %get-tuple-element.29.refs_0_.refs_2_.refs_8_.refs_24_), channel_id=1, source_target_pairs={{0,16},{4,20},{8,24},{12,28},{16,0},{20,4},{24,8},{28,12},{1,17},{... | collective-permute-start | bytes 1253384 | tf_op jit(solution)/shard_map/ppermute | solution.py:360
  9.1 15.9 %collective-permute-start.15 = (bf16[256,1024]{1,0:T(8,128)(2,1)}, bf16[256,1024]{1,0:T(8,128)(2,1)}, u32[]{:S(2)}, u32[]{:S(2)}) collective-permute-start(bf16[256,1024]{1,0:T(8,128)(2,1)} %shard_map.84.refs_0_), channel_id=1, source_target_pairs={{0,1},{1,0},{2,3},{3,2},{4,5},{5,4},{6,7},{7,6},{8,9},{9,8},{10,11... | collective-permute-start | bytes 1572872 | tf_op jit(solution)/shard_map/ppermute | solution.py:375
  10.7 12.8 %collective-permute-start.1 = (bf16[136,1536]{1,0:T(8,128)(2,1)}, bf16[136,1536]{1,0:T(8,128)(2,1)}, u32[]{:S(2)}, u32[]{:S(2)}) collective-permute-start(bf16[136,1536]{1,0:T(8,128)(2,1)} %get-tuple-element.29.refs_0_.refs_2_.refs_8_.refs_24_), channel_id=1, source_target_pairs={{0,8},{4,12},{8,0},{12,4},{16,24},{20,28},{24,16},{28,20},{1,9},{5... | collective-permute-start | bytes 1253384 | tf_op jit(solution)/shard_map/ppermute | solution.py:360
  12.2 14.3 %collective-permute-start.4 = (bf16[136,1536]{1,0:T(8,128)(2,1)}, bf16[136,1536]{1,0:T(8,128)(2,1)}, u32[]{:S(2)}, u32[]{:S(2)}) collective-permute-start(bf16[136,1536]{1,0:T(8,128)(2,1)} %get-tuple-element.30.refs_1_.refs_3_.refs_9_.refs_25_), channel_id=1, source_target_pairs={{0,16},{4,20},{8,24},{12,28},{16,0},{20,4},{24,8},{28,12},{1,17},{... | collective-permute-start | bytes 1253384 | tf_op jit(solution)/shard_map/ppermute | solution.py:360
  17.6 14.7 %collective-permute-start.2 = (bf16[136,1536]{1,0:T(8,128)(2,1)}, bf16[136,1536]{1,0:T(8,128)(2,1)S(1)}, u32[]{:S(2)}, u32[]{:S(2)}) collective-permute-start(bf16[136,1536]{1,0:T(8,128)(2,1)} %get-tuple-element.30.refs_1_.refs_3_.refs_9_.refs_25_), channel_id=1, source_target_pairs={{0,8},{4,12},{8,0},{12,4},{16,24},{20,28},{24,16},{28,20},{1,9},{5... | collective-permute-start | bytes 1253384 | tf_op jit(solution)/shard_map/ppermute | solution.py:360
  23.5 27.0 %collective-permute-start.16 = (bf16[256,1024]{1,0:T(8,128)(2,1)}, bf16[256,1024]{1,0:T(8,128)(2,1)}, u32[]{:S(2)}, u32[]{:S(2)}) collective-permute-start(bf16[256,1024]{1,0:T(8,128)(2,1)} %shard_map.84.refs_0_), channel_id=1, source_target_pairs={{1,2},{2,1},{5,6},{6,5},{9,10},{10,9},{13,14},{14,13},{17,18},{18,... | collective-permute-start | bytes 1572872 | tf_op jit(solution)/shard_map/ppermute | solution.py:375
  25.0 26.8 %collective-permute-start.18 = (bf16[256,1024]{1,0:T(8,128)(2,1)}, bf16[256,1024]{1,0:T(8,128)(2,1)}, u32[]{:S(2)}, u32[]{:S(2)}) collective-permute-start(bf16[256,1024]{1,0:T(8,128)(2,1)} %collective-permute-done.15.refs_1_), channel_id=1, source_target_pairs={{1,2},{2,1},{5,6},{6,5},{9,10},{10,9},{13,14},{14,13},{17,18},{18,... | collective-permute-start | bytes 1572872 | tf_op jit(solution)/shard_map/ppermute | solution.py:375
  26.5 15.8 %collective-permute-start.7 = (bf16[136,1536]{1,0:T(8,128)(2,1)S(1)}, bf16[136,1536]{1,0:T(8,128)(2,1)S(1)}, u32[]{:S(2)}, u32[]{:S(2)}) collective-permute-start(bf16[136,1536]{1,0:T(8,128)(2,1)S(1)} %collective-permute-done.3.refs_2_.refs_5_.refs_12_.refs_28_), channel_id=1, source_target_pairs={{0,8},{4,12},{8,0},{12,4},{16,24},{20,28},{24,16},{28,20},{1,9},{5... | collective-permute-start | bytes 1253384 | tf_op jit(solution)/shard_map/ppermute | solution.py:360
  40.8 14.7 %collective-permute-start.5 = (bf16[256,1024]{1,0:T(8,128)(2,1)}, bf16[256,1024]{1,0:T(8,128)(2,1)S(1)}, u32[]{:S(2)}, u32[]{:S(2)}) collective-permute-start(bf16[256,1024]{1,0:T(8,128)(2,1)} %get-tuple-element.31), channel_id=1, source_target_pairs={{0,8},{4,12},{8,0},{12,4},{16,24},{20,28},{24,16},{28,20},{1,9},{5... | collective-permute-start | bytes 1572872 | tf_op jit(solution)/shard_map/ppermute | solution.py:360
  42.3 23.0 %collective-permute-start.6 = (bf16[256,1024]{1,0:T(8,128)(2,1)}, bf16[256,1024]{1,0:T(8,128)(2,1)S(1)}, u32[]{:S(2)}, u32[]{:S(2)}) collective-permute-start(bf16[256,1024]{1,0:T(8,128)(2,1)} %get-tuple-element.32), channel_id=1, source_target_pairs={{0,16},{4,20},{8,24},{12,28},{16,0},{20,4},{24,8},{28,12},{1,17},{... | collective-permute-start | bytes 1572872 | tf_op jit(solution)/shard_map/ppermute | solution.py:360
  49.8 22.0 %collective-permute-start.9 = (bf16[256,1024]{1,0:T(8,128)(2,1)}, bf16[256,1024]{1,0:T(8,128)(2,1)S(1)}, u32[]{:S(2)}, u32[]{:S(2)}) collective-permute-start(bf16[256,1024]{1,0:T(8,128)(2,1)} %shard_map.79), channel_id=1, source_target_pairs={{0,24},{4,28},{8,16},{12,20},{16,8},{20,12},{24,0},{28,4},{1,25},{... | collective-permute-start | bytes 1572872 | tf_op jit(solution)/shard_map/ppermute | solution.py:360
  50.5 26.6 %collective-permute-start.17 = (bf16[256,1024]{1,0:T(8,128)(2,1)}, bf16[256,1024]{1,0:T(8,128)(2,1)}, u32[]{:S(2)}, u32[]{:S(2)}) collective-permute-start(bf16[256,1024]{1,0:T(8,128)(2,1)} %collective-permute-done.16.refs_2_), channel_id=1, source_target_pairs={{1,0},{2,3},{5,4},{6,7},{9,8},{10,11},{13,12},{14,15},{17,16},{18,... | collective-permute-start | bytes 1572872 | tf_op jit(solution)/shard_map/ppermute | solution.py:375
  51.8 25.8 %collective-permute-start.19 = (bf16[256,1024]{1,0:T(8,128)(2,1)}, bf16[256,1024]{1,0:T(8,128)(2,1)}, u32[]{:S(2)}, u32[]{:S(2)}) collective-permute-start(bf16[256,1024]{1,0:T(8,128)(2,1)} %collective-permute-done.18.refs_4_), channel_id=1, source_target_pairs={{1,0},{2,3},{5,4},{6,7},{9,8},{10,11},{13,12},{14,15},{17,16},{18,... | collective-permute-start | bytes 1572872 | tf_op jit(solution)/shard_map/ppermute | solution.py:375
  55.5 21.6 %collective-permute-start.33 = (bf16[136,1536]{1,0:T(8,128)(2,1)}, bf16[136,1536]{1,0:T(8,128)(2,1)}, u32[]{:S(2)}, u32[]{:S(2)}) collective-permute-start(bf16[136,1536]{1,0:T(8,128)(2,1)} %get-tuple-element.29.refs_0_.refs_2_.refs_8_.refs_24_), channel_id=1, source_target_pairs={{0,4},{4,0},{8,12},{12,8},{16,20},{20,16},{24,28},{28,24},{1,5},{5... | collective-permute-start | bytes 1253384 | tf_op jit(solution)/shard_map/ppermute | solution.py:363
  65.3 15.9 %collective-permute-start.34 = (bf16[136,1536]{1,0:T(8,128)(2,1)}, bf16[136,1536]{1,0:T(8,128)(2,1)}, u32[]{:S(2)}, u32[]{:S(2)}) collective-permute-start(bf16[136,1536]{1,0:T(8,128)(2,1)} %get-tuple-element.30.refs_1_.refs_3_.refs_9_.refs_25_), channel_id=1, source_target_pairs={{0,4},{4,0},{8,12},{12,8},{16,20},{20,16},{24,28},{28,24},{1,5},{5... | collective-permute-start | bytes 1253384 | tf_op jit(solution)/shard_map/ppermute | solution.py:363
  74.5 14.5 %collective-permute-start.10 = (bf16[256,1024]{1,0:T(8,128)(2,1)}, bf16[256,1024]{1,0:T(8,128)(2,1)S(1)}, u32[]{:S(2)}, u32[]{:S(2)}) collective-permute-start(bf16[256,1024]{1,0:T(8,128)(2,1)} %shard_map.80), channel_id=1, source_target_pairs={{0,1},{3,2},{4,5},{7,6},{8,9},{11,10},{12,13},{15,14},{16,17},{19,... | collective-permute-start | bytes 1572872 | tf_op jit(solution)/shard_map/ppermute | solution.py:375
  81.2 20.6 %collective-permute-start.23 = (bf16[256,1024]{1,0:T(8,128)(2,1)}, bf16[256,1024]{1,0:T(8,128)(2,1)S(1)}, u32[]{:S(2)}, u32[]{:S(2)}) collective-permute-start(bf16[256,1024]{1,0:T(8,128)(2,1)} %get-tuple-element.43), channel_id=1, source_target_pairs={{0,24},{4,28},{8,16},{12,20},{16,8},{20,12},{24,0},{28,4},{1,25},{... | collective-permute-start | bytes 1572872 | tf_op jit(solution)/shard_map/ppermute | solution.py:360
  89.0 19.1 %collective-permute-start.20 = (bf16[256,1024]{1,0:T(8,128)(2,1)}, bf16[256,1024]{1,0:T(8,128)(2,1)S(1)}, u32[]{:S(2)}, u32[]{:S(2)}) collective-permute-start(bf16[256,1024]{1,0:T(8,128)(2,1)} %get-tuple-element.39), channel_id=1, source_target_pairs={{0,8},{4,12},{8,0},{12,4},{16,24},{20,28},{24,16},{28,20},{1,9},{5... | collective-permute-start | bytes 1572872 | tf_op jit(solution)/shard_map/ppermute | solution.py:360
  91.8 17.5 %collective-permute-start.21 = (bf16[256,1024]{1,0:T(8,128)(2,1)}, bf16[256,1024]{1,0:T(8,128)(2,1)S(1)}, u32[]{:S(2)}, u32[]{:S(2)}) collective-permute-start(bf16[256,1024]{1,0:T(8,128)(2,1)} %get-tuple-element.40), channel_id=1, source_target_pairs={{0,16},{4,20},{8,24},{12,28},{16,0},{20,4},{24,8},{28,12},{1,17},{... | collective-permute-start | bytes 1572872 | tf_op jit(solution)/shard_map/ppermute | solution.py:360
  92.9 16.5 %collective-permute-start.11 = (bf16[256,1024]{1,0:T(8,128)(2,1)}, bf16[256,1024]{1,0:T(8,128)(2,1)S(1)}, u32[]{:S(2)}, u32[]{:S(2)}) collective-permute-start(bf16[256,1024]{1,0:T(8,128)(2,1)} %get-tuple-element.33), channel_id=1, source_target_pairs={{2,1},{1,2},{6,5},{5,6},{10,9},{9,10},{14,13},{13,14},{18,17},{17,... | collective-permute-start | bytes 1572872 | tf_op jit(solution)/shard_map/ppermute | solution.py:375
  93.6 18.7 %collective-permute-start.12 = (bf16[256,1024]{1,0:T(8,128)(2,1)}, bf16[256,1024]{1,0:T(8,128)(2,1)S(1)}, u32[]{:S(2)}, u32[]{:S(2)}) collective-permute-start(bf16[256,1024]{1,0:T(8,128)(2,1)} %get-tuple-element.34), channel_id=1, source_target_pairs={{0,1},{3,2},{4,5},{7,6},{8,9},{11,10},{12,13},{15,14},{16,17},{19,... | collective-permute-start | bytes 1572872 | tf_op jit(solution)/shard_map/ppermute | solution.py:375
  101.8 15.0 %collective-permute-start.29 = (bf16[256,1024]{1,0:T(8,128)(2,1)}, bf16[256,1024]{1,0:T(8,128)(2,1)}, u32[]{:S(2)}, u32[]{:S(2)}) collective-permute-start(bf16[256,1024]{1,0:T(8,128)(2,1)} %get-tuple-element.37.refs_0_.refs_1_), channel_id=1, source_target_pairs={{0,4},{4,0},{8,12},{12,8},{16,20},{20,16},{24,28},{28,24},{1,5},{5... | collective-permute-start | bytes 1572872 | tf_op jit(solution)/shard_map/ppermute | solution.py:363
  109.3 22.7 %collective-permute-start.30 = (bf16[256,1024]{1,0:T(8,128)(2,1)S(1)}, bf16[256,1024]{1,0:T(8,128)(2,1)S(1)}, u32[]{:S(2)}, u32[]{:S(2)}) collective-permute-start(bf16[256,1024]{1,0:T(8,128)(2,1)S(1)} %collective-permute-done.20.refs_0_.refs_2_.refs_1_), channel_id=1, source_target_pairs={{0,4},{4,0},{8,12},{12,8},{16,20},{20,16},{24,28},{28,24},{1,5},{5... | collective-permute-start | bytes 1572872 | tf_op jit(solution)/shard_map/ppermute | solution.py:363
  109.4 24.2 %collective-permute-start.31 = (bf16[256,1024]{1,0:T(8,128)(2,1)S(1)}, bf16[256,1024]{1,0:T(8,128)(2,1)S(1)}, u32[]{:S(2)}, u32[]{:S(2)}) collective-permute-start(bf16[256,1024]{1,0:T(8,128)(2,1)S(1)} %collective-permute-done.21.refs_1_.refs_3_.refs_2_), channel_id=1, source_target_pairs={{0,4},{4,0},{8,12},{12,8},{16,20},{20,16},{24,28},{28,24},{1,5},{5... | collective-permute-start | bytes 1572872 | tf_op jit(solution)/shard_map/ppermute | solution.py:363
  116.8 17.8 %collective-permute-start.32 = (bf16[256,1024]{1,0:T(8,128)(2,1)S(1)}, bf16[256,1024]{1,0:T(8,128)(2,1)S(1)}, u32[]{:S(2)}, u32[]{:S(2)}) collective-permute-start(bf16[256,1024]{1,0:T(8,128)(2,1)S(1)} %collective-permute-done.23.refs_0_.refs_1_.refs_3_), channel_id=1, source_target_pairs={{0,4},{4,0},{8,12},{12,8},{16,20},{20,16},{24,28},{28,24},{1,5},{5... | collective-permute-start | bytes 1572872 | tf_op jit(solution)/shard_map/ppermute | solution.py:363
  119.8 15.9 %collective-permute-start.13 = (bf16[256,1024]{1,0:T(8,128)(2,1)}, bf16[256,1024]{1,0:T(8,128)(2,1)S(1)}, u32[]{:S(2)}, u32[]{:S(2)}) collective-permute-start(bf16[256,1024]{1,0:T(8,128)(2,1)} %get-tuple-element.35), channel_id=1, source_target_pairs={{1,0},{0,1},{3,2},{2,3},{5,4},{4,5},{7,6},{6,7},{9,8},{8,9},{11,10... | collective-permute-start | bytes 1572872 | tf_op jit(solution)/shard_map/ppermute | solution.py:375
  121.6 32.8 %collective-permute-start.14 = (bf16[256,1024]{1,0:T(8,128)(2,1)}, bf16[256,1024]{1,0:T(8,128)(2,1)S(1)}, u32[]{:S(2)}, u32[]{:S(2)}) collective-permute-start(bf16[256,1024]{1,0:T(8,128)(2,1)} %get-tuple-element.36), channel_id=1, source_target_pairs={{2,1},{1,2},{6,5},{5,6},{10,9},{9,10},{14,13},{13,14},{18,17},{17,... | collective-permute-start | bytes 1572872 | tf_op jit(solution)/shard_map/ppermute | solution.py:375
  132.0 24.4 %collective-permute-start.22 = (bf16[128,1536]{1,0:T(8,128)(2,1)}, bf16[128,1536]{1,0:T(8,128)(2,1)S(1)}, u32[]{:S(2)}, u32[]{:S(2)}) collective-permute-start(bf16[128,1536]{1,0:T(8,128)(2,1)} %get-tuple-element.41), channel_id=1, source_target_pairs={{0,8},{4,12},{8,0},{12,4},{16,24},{20,28},{24,16},{28,20},{1,9},{5... | collective-permute-start | bytes 1179656 | tf_op jit(solution)/shard_map/ppermute | solution.py:360
  133.6 22.8 %collective-permute-start.28 = (bf16[128,1536]{1,0:T(8,128)(2,1)}, bf16[128,1536]{1,0:T(8,128)(2,1)S(1)}, u32[]{:S(2)}, u32[]{:S(2)}) collective-permute-start(bf16[128,1536]{1,0:T(8,128)(2,1)} %get-tuple-element.50), channel_id=1, source_target_pairs={{0,16},{4,20},{8,24},{12,28},{16,0},{20,4},{24,8},{28,12},{1,17},{... | collective-permute-start | bytes 1179656 | tf_op jit(solution)/shard_map/ppermute | solution.py:360
  134.6 21.8 %collective-permute-start.26 = (bf16[128,1536]{1,0:T(8,128)(2,1)}, bf16[128,1536]{1,0:T(8,128)(2,1)S(1)}, u32[]{:S(2)}, u32[]{:S(2)}) collective-permute-start(bf16[128,1536]{1,0:T(8,128)(2,1)} %get-tuple-element.47), channel_id=1, source_target_pairs={{0,16},{4,20},{8,24},{12,28},{16,0},{20,4},{24,8},{28,12},{1,17},{... | collective-permute-start | bytes 1179656 | tf_op jit(solution)/shard_map/ppermute | solution.py:360
  135.7 20.8 %collective-permute-start.27 = (bf16[128,1536]{1,0:T(8,128)(2,1)}, bf16[128,1536]{1,0:T(8,128)(2,1)S(1)}, u32[]{:S(2)}, u32[]{:S(2)}) collective-permute-start(bf16[128,1536]{1,0:T(8,128)(2,1)} %get-tuple-element.49), channel_id=1, source_target_pairs={{0,8},{4,12},{8,0},{12,4},{16,24},{20,28},{24,16},{28,20},{1,9},{5... | collective-permute-start | bytes 1179656 | tf_op jit(solution)/shard_map/ppermute | solution.py:360
  (31 other events, 331.6 us)

commit v3 on v2

--- a/solution.py
+++ b/solution.py
@@ -14,6 +14,7 @@
 KIND_ROWS = 8
 PART_KINDS = ((0, 1), (2, 1))
 PROJECT_TILE = 512
+SMALL_PROJECT_TILE = 768
 WEIGHT_TILE = 512
 
 
@@ -177,7 +178,7 @@
 
 def project_parts(core, items, own_weight, other_weight):
     kinds, half, columns = own_weight.shape
-    tile = math.gcd(columns, PROJECT_TILE)
+    tile = math.gcd(columns, PROJECT_TILE if len(items) > 2 else SMALL_PROJECT_TILE)
     weight_spec = pl.BlockSpec((kinds, half, tile), lambda step, core: (0, 0, step))
     cut = items[0][2].shape[0] - KIND_ROWS
     return pl.pallas_call(
@@ -192,7 +193,7 @@
         ),
         out_shape=[pltpu.HBM((cut, columns), BF16)] * len(items),
         compiler_params=limit(28),
-    )(core, *in_hbm(own_weight, other_weight), *[item[0] for item in items], *in_hbm(*[item[2] for item in items]))
+    )(core, *in_hbm(own_weight, other_weight, *[item[0] for item in items], *[item[2] for item in items]))
 
 
 def total_kernel(*refs, counts):
@@ -410,7 +411,7 @@
         )
         for offset, term in zip(group, made):
             arrived[offset] = across(term, offset) if offset else term
-    all_terms = in_hbm(*[arrived[offset] for offset in range(chip_count)])
+    all_terms = [arrived[offset] for offset in range(chip_count)]
 
     def term_number(where):
         return chip ^ jnp.clip(where, 0, tp_count - 1)

time: 163 us -> 161 us (0.988)
  Pallas kernels: 75.1 us -> 70.5 us
  starting transfers between devices: 42.6 us -> 44.8 us
    pallas_call x5, Pallas kernels: 12.8 us -> 8.83 us  [fold(): pl.pallas_call(functools.partial(fold_kernel, sources=len(sources), count...]
    ppermute x18, starting transfers between devices: 20.3 us -> 22.9 us  [across(): return lax.ppermute(value, 'loop', pairs)]
  transfers between devices with their start and end apart: 41 -> 41, of which waited for: 10 -> 10; matrix products, arithmetic and copies ran while one was open for 0% -> 0% of each run, Pallas kernels for 45% -> 42%
where the time goes in v3:
time: 161 us; the launch traced here: 159 us
  Pallas kernels  70.5 us (44%)
  starting transfers between devices  44.8 us (28%)
  waiting for transfers between devices  39.4 us (24%)
  local copies, waits for them, and re-layouts  3.06 us (2%)
    ppermute x18, waiting for transfers between devices, across(): return lax.ppermute(value, 'loop', pairs)  31.2 us
    ppermute x18, starting transfers between devices, across(): return lax.ppermute(value, 'loop', pairs)  22.9 us
    pallas_call x3, Pallas kernels, input_terms(): pl.pallas_call(functools.partial(input_kernel, blocks=len(blocks), tile=t...  20.1 us
    ppermute x10, starting transfers between devices, along(): return lax.ppermute(value, 'tp', pairs)  19.2 us
    pallas_call x3, Pallas kernels, project_parts(): pl.pallas_call(functools.partial(project_kernel, items=len(items)), grid_...  18.8 us
    pallas_call x1, Pallas kernels, weight_gradient(): pl.pallas_call(functools.partial(weight_kernel, blocks=len(blocks), grads...  12 us
    pallas_call x5, Pallas kernels, fold(): pl.pallas_call(functools.partial(fold_kernel, sources=len(sources), count...  8.83 us
    ppermute x10, waiting for transfers between devices, along(): return lax.ppermute(value, 'tp', pairs)  8.23 us
  transfers between devices with their start and end apart: 41, of which 10 were waited for; matrix products, arithmetic and copies ran while one was open for 0% of the time, Pallas kernels for 42%

profile of v3, /device:TPU:0, one launch (start us, length us, event | category | flops | bytes accessed | tf_op | source)
XLA Modules:
  0.0 158.9 jit_solution(14315068250245530245)
XLA Ops:
  1.2 3.2 %shard_map.76 = (bf16[136,1536]{1,0:T(8,128)(2,1)}, bf16[136,1536]{1,0:T(8,128)(2,1)}, f32[8,256]{1,0:T(8,128)}) custom-call(s32[8]{0:T(128)} %kinds_of_loops.1, s32[1,256]{1,0:T(1,128)} %bitcast.12, bf16[256,1536]{1,0:T(8,128)(2,1)} %grads.1), custom_call_target="tpu_custom_call" | custom-call | tf_op jit(solution)/shard_map/pallas_call | solution.py:62
  4.4 2.5 %collective-permute-start.3 = (bf16[136,1536]{1,0:T(8,128)(2,1)}, bf16[136,1536]{1,0:T(8,128)(2,1)}, u32[]{:S(2)}, u32[]{:S(2)}) collective-permute-start(bf16[136,1536]{1,0:T(8,128)(2,1)} %get-tuple-element.29.refs_0_.refs_2_.refs_8_.refs_24_), channel_id=1, source_target_pairs={{0,16},{4,20},{8,24},{12,28},{16,0},{20,4},{24,8},{28,12},{1,17},{... | collective-permute-start | bytes 1253384 | tf_op jit(solution)/shard_map/ppermute | solution.py:361
  6.9 2.2 %shard_map.84.refs_0_ = bf16[256,1024]{1,0:T(8,128)(2,1)} custom-call(f32[8,256]{1,0:T(8,128)} %get-tuple-element.28.places, bf16[256,1024]{1,0:T(8,128)(2,1)} %rows.1), custom_call_target="tpu_custom_call" | custom-call | tf_op jit(solution)/shard_map/pallas_call | solution.py:82
  9.1 1.6 collective-permute-start.15
  12.7 5.1 %collective-permute-done.3.refs_2_.refs_5_.refs_12_.refs_28_ = bf16[136,1536]{1,0:T(8,128)(2,1)} collective-permute-done((bf16[136,1536]{1,0:T(8,128)(2,1)}, bf16[136,1536]{1,0:T(8,128)(2,1)}, u32[]{:S(2)}, u32[]{:S(2)}) %collective-permute-start.3) | collective-permute-done | bytes 417824 | tf_op jit(solution)/shard_map/ppermute | solution.py:361
  17.8 2.0 %collective-permute-start.2 = (bf16[136,1536]{1,0:T(8,128)(2,1)}, bf16[136,1536]{1,0:T(8,128)(2,1)}, u32[]{:S(2)}, u32[]{:S(2)}) collective-permute-start(bf16[136,1536]{1,0:T(8,128)(2,1)} %get-tuple-element.30.refs_1_.refs_3_.refs_9_.refs_25_), channel_id=1, source_target_pairs={{0,8},{4,12},{8,0},{12,4},{16,24},{20,28},{24,16},{28,20},{1,9},{5... | collective-permute-start | bytes 1253384 | tf_op jit(solution)/shard_map/ppermute | solution.py:361
  19.7 3.8 %collective-permute-done.1.refs_0_.refs_4_.refs_10_.refs_26_ = bf16[136,1536]{1,0:T(8,128)(2,1)} collective-permute-done((bf16[136,1536]{1,0:T(8,128)(2,1)}, bf16[136,1536]{1,0:T(8,128)(2,1)}, u32[]{:S(2)}, u32[]{:S(2)}) %collective-permute-start.1) | collective-permute-done | bytes 417824 | tf_op jit(solution)/shard_map/ppermute | solution.py:361
  26.5 1.7 %collective-permute-start.7 = (bf16[136,1536]{1,0:T(8,128)(2,1)}, bf16[136,1536]{1,0:T(8,128)(2,1)S(1)}, u32[]{:S(2)}, u32[]{:S(2)}) collective-permute-start(bf16[136,1536]{1,0:T(8,128)(2,1)} %collective-permute-done.3.refs_2_.refs_5_.refs_12_.refs_28_), channel_id=1, source_target_pairs={{0,8},{4,12},{8,0},{12,4},{16,24},{20,28},{24,16},{28,20},{1,9},{5... | collective-permute-start | bytes 1253384 | tf_op jit(solution)/shard_map/ppermute | solution.py:361
  28.2 4.2 %collective-permute-done.2.refs_1_.refs_6_.refs_11_.refs_27_ = bf16[136,1536]{1,0:T(8,128)(2,1)} collective-permute-done((bf16[136,1536]{1,0:T(8,128)(2,1)}, bf16[136,1536]{1,0:T(8,128)(2,1)}, u32[]{:S(2)}, u32[]{:S(2)}) %collective-permute-start.2) | collective-permute-done | bytes 417824 | tf_op jit(solution)/shard_map/ppermute | solution.py:361
  33.0 7.6 %shard_map.78 = (bf16[256,1024]{1,0:T(8,128)(2,1)}, bf16[256,1024]{1,0:T(8,128)(2,1)}) custom-call(s32[1]{0:T(128)} %bitcast.2.core, bf16[3,512,1536]{2,1,0:T(8,128)(2,1)} %own_weight.11, bf16[3,512,1536]{2,1,0:T(8,128)(2,1)} %collective-permute-done.other_weight, bf16[136,1536]{1,0:T(8,128)(2,1)} %collective-permute-done.1.refs_0_.refs_4_.refs_10_.refs_26_, ...), custom_call_target="tpu_custom_call" | custom-call | tf_op jit(solution)/shard_map/pallas_call | solution.py:140
  42.1 1.5 collective-permute-start.6
  43.6 6.2 %shard_map.79 = bf16[256,1024]{1,0:T(8,128)(2,1)} custom-call(s32[1]{0:T(128)} %bitcast.2.core, bf16[3,512,1536]{2,1,0:T(8,128)(2,1)} %own_weight.11, bf16[3,512,1536]{2,1,0:T(8,128)(2,1)} %collective-permute-done.other_weight, bf16[136,1536]{1,0:T(8,128)(2,1)S(1)} %collective-permute-done.7.refs_0_.refs_2_.refs_14_.refs_30_, ...), custom_call_target="tpu_custom_call" | custom-call | tf_op jit(solution)/shard_map/pallas_call | solution.py:140
  52.9 2.1 %collective-permute-done.5.refs_1_ = bf16[256,1024]{1,0:T(8,128)(2,1)S(1)} collective-permute-done((bf16[256,1024]{1,0:T(8,128)(2,1)}, bf16[256,1024]{1,0:T(8,128)(2,1)S(1)}, u32[]{:S(2)}, u32[]{:S(2)}) %collective-permute-start.5) | collective-permute-done | bytes 524320 | tf_op jit(solution)/shard_map/ppermute | solution.py:361
  55.0 9.8 %collective-permute-done.6.refs_2_ = bf16[256,1024]{1,0:T(8,128)(2,1)S(1)} collective-permute-done((bf16[256,1024]{1,0:T(8,128)(2,1)}, bf16[256,1024]{1,0:T(8,128)(2,1)S(1)}, u32[]{:S(2)}, u32[]{:S(2)}) %collective-permute-start.6) | collective-permute-done | bytes 524320 | tf_op jit(solution)/shard_map/ppermute | solution.py:361
  64.8 6.3 %shard_map.77.refs_0_ = bf16[256,1024]{1,0:T(8,128)(2,1)} custom-call(s32[1]{0:T(128)} %bitcast.2.core, bf16[3,512,1536]{2,1,0:T(8,128)(2,1)} %own_weight.11, bf16[3,512,1536]{2,1,0:T(8,128)(2,1)} %collective-permute-done.other_weight, bf16[136,1536]{1,0:T(8,128)(2,1)} %get-tuple-element.29.refs_0_.refs_2_.refs_8_.refs_24_, ...), custom_call_target="tpu_custom_call" | custom-call | tf_op jit(solution)/shard_map/pallas_call | solution.py:140
  73.0 2.3 %collective-permute-start.10 = (bf16[256,1024]{1,0:T(8,128)(2,1)}, bf16[256,1024]{1,0:T(8,128)(2,1)S(1)}, u32[]{:S(2)}, u32[]{:S(2)}) collective-permute-start(bf16[256,1024]{1,0:T(8,128)(2,1)} %shard_map.80), channel_id=1, source_target_pairs={{0,1},{3,2},{4,5},{7,6},{8,9},{11,10},{12,13},{15,14},{16,17},{19,... | collective-permute-start | bytes 1572872 | tf_op jit(solution)/shard_map/ppermute | solution.py:376
  76.2 3.4 %shard_map.85 = (bf16[256,1024]{1,0:T(8,128)(2,1)}, bf16[256,1024]{1,0:T(8,128)(2,1)}, bf16[256,1024]{1,0:T(8,128)(2,1)}, bf16[256,1024]{1,0:T(8,128)(2,1)}) custom-call(s32[4]{0:T(128)S(1)} %pad_add_fusion.2.wanted, bf16[256,1024]{1,0:T(8,128)(2,1)} %shard_map.84.refs_0_, bf16[256,1024]{1,0:T(8,128)(2,1)} %copy-done.9, ...), custom_call_target="tpu_custom_call" | custom-call | tf_op jit(solution)/shard_map/pallas_call | solution.py:274
  79.7 1.6 %collective-permute-start.23 = (bf16[256,1024]{1,0:T(8,128)(2,1)}, bf16[256,1024]{1,0:T(8,128)(2,1)}, u32[]{:S(2)}, u32[]{:S(2)}) collective-permute-start(bf16[256,1024]{1,0:T(8,128)(2,1)} %get-tuple-element.43), channel_id=1, source_target_pairs={{0,24},{4,28},{8,16},{12,20},{16,8},{20,12},{24,0},{28,4},{1,25},{... | collective-permute-start | bytes 1572872 | tf_op jit(solution)/shard_map/ppermute | solution.py:361
  81.9 5.5 %collective-permute-done.10.refs_4_ = bf16[256,1024]{1,0:T(8,128)(2,1)S(1)} collective-permute-done((bf16[256,1024]{1,0:T(8,128)(2,1)}, bf16[256,1024]{1,0:T(8,128)(2,1)S(1)}, u32[]{:S(2)}, u32[]{:S(2)}) %collective-permute-start.10) | collective-permute-done | bytes 524320 | tf_op jit(solution)/shard_map/ppermute | solution.py:376
  89.0 1.7 %shard_map.81 = (bf16[256,1024]{1,0:T(8,128)(2,1)}, bf16[256,1024]{1,0:T(8,128)(2,1)}) custom-call(s32[2]{0:T(128)S(1)} %pad_add_fusion.1.wanted, bf16[256,1024]{1,0:T(8,128)(2,1)S(1)} %copy-done.1, bf16[256,1024]{1,0:T(8,128)(2,1)S(1)} %collective-permute-done.5.refs_1_, bf16[256,1024]{1,0:T(8,128)(2,1)S(1)} %collective-permute-done.6.refs_2_, ...), custom_call_target="tpu_custom_call" | custom-call | tf_op jit(solution)/shard_map/pallas_call | solution.py:274
  92.2 8.2 %collective-permute-start.12 = (bf16[256,1024]{1,0:T(8,128)(2,1)}, bf16[256,1024]{1,0:T(8,128)(2,1)S(1)}, u32[]{:S(2)}, u32[]{:S(2)}) collective-permute-start(bf16[256,1024]{1,0:T(8,128)(2,1)} %get-tuple-element.34), channel_id=1, source_target_pairs={{0,1},{3,2},{4,5},{7,6},{8,9},{11,10},{12,13},{15,14},{16,17},{19,... | collective-permute-start | bytes 1572872 | tf_op jit(solution)/shard_map/ppermute | solution.py:376
  100.5 5.8 %shard_map.88 = (bf16[128,1536]{1,0:T(8,128)(2,1)}, bf16[128,1536]{1,0:T(8,128)(2,1)}) custom-call(s32[1]{0:T(128)} %bitcast.2.core, bf16[3,512,1536]{2,1,0:T(8,128)(2,1)} %own_weight.11, bf16[3,512,1536]{2,1,0:T(8,128)(2,1)} %collective-permute-done.other_weight, bf16[256,1024]{1,0:T(8,128)(2,1)} %collective-permute-done.23.refs_0_.refs_1_.refs_3_, ...), custom_call_target="tpu_custom_call" | custom-call | tf_op jit(solution)/shard_map/pallas_call | solution.py:184
  108.3 2.7 %collective-permute-done.12.refs_5_ = bf16[256,1024]{1,0:T(8,128)(2,1)S(1)} collective-permute-done((bf16[256,1024]{1,0:T(8,128)(2,1)}, bf16[256,1024]{1,0:T(8,128)(2,1)S(1)}, u32[]{:S(2)}, u32[]{:S(2)}) %collective-permute-start.12) | collective-permute-done | bytes 524320 | tf_op jit(solution)/shard_map/ppermute | solution.py:376
  112.4 1.8 %shard_map.82 = (bf16[256,1024]{1,0:T(8,128)(2,1)}, bf16[256,1024]{1,0:T(8,128)(2,1)}) custom-call(s32[2]{0:T(128)S(1)} %pad_add_fusion.wanted, bf16[256,1024]{1,0:T(8,128)(2,1)S(1)} %copy-done.1, bf16[256,1024]{1,0:T(8,128)(2,1)S(1)} %collective-permute-done.5.refs_1_, bf16[256,1024]{1,0:T(8,128)(2,1)S(1)} %collective-permute-done.6.refs_2_, ...), custom_call_target="tpu_custom_call" | custom-call | tf_op jit(solution)/shard_map/pallas_call | solution.py:274
  114.3 3.8 %collective-permute-done.24.refs_1_ = bf16[128,1536]{1,0:T(8,128)(2,1)} collective-permute-done((bf16[128,1536]{1,0:T(8,128)(2,1)}, bf16[128,1536]{1,0:T(8,128)(2,1)}, u32[]{:S(2)}, u32[]{:S(2)}) %collective-permute-start.24) | collective-permute-done | bytes 393248 | tf_op jit(solution)/shard_map/ppermute | solution.py:361
  118.1 2.1 %collective-permute-done.25.refs_3_ = bf16[128,1536]{1,0:T(8,128)(2,1)S(1)} collective-permute-done((bf16[128,1536]{1,0:T(8,128)(2,1)}, bf16[128,1536]{1,0:T(8,128)(2,1)S(1)}, u32[]{:S(2)}, u32[]{:S(2)}) %collective-permute-start.25) | collective-permute-done | bytes 393248 | tf_op jit(solution)/shard_map/ppermute | solution.py:361
  121.1 7.4 %shard_map.87 = (bf16[128,1536]{1,0:T(8,128)(2,1)}, bf16[128,1536]{1,0:T(8,128)(2,1)}, bf16[128,1536]{1,0:T(8,128)(2,1)}, bf16[128,1536]{1,0:T(8,128)(2,1)}) custom-call(s32[1]{0:T(128)} %bitcast.2.core, bf16[3,512,1536]{2,1,0:T(8,128)(2,1)} %own_weight.11, bf16[3,512,1536]{2,1,0:T(8,128)(2,1)} %collective-permute-done.other_weight, ...), custom_call_target="tpu_custom_call" | custom-call | tf_op jit(solution)/shard_map/pallas_call | solution.py:184
  128.5 2.3 %shard_map.89 = (bf16[128,1536]{1,0:T(8,128)(2,1)}, bf16[128,1536]{1,0:T(8,128)(2,1)}) custom-call(bf16[128,1536]{1,0:T(8,128)(2,1)} %get-tuple-element.42.refs_0_, bf16[128,1536]{1,0:T(8,128)(2,1)} %collective-permute-done.24.refs_1_, bf16[128,1536]{1,0:T(8,128)(2,1)} %get-tuple-element.45.refs_2_, bf16[128,1536]{1,0:T(8,128)(2,1)} %copy-done.10), custom_call_target="tpu_custom_call" | custom-call | tf_op jit(solution)/shard_map/pallas_call | solution.py:212
  132.8 1.5 collective-permute-start.26
  135.0 12.0 %shard_map.91 = bf16[3,512,1536]{2,1,0:T(8,128)(2,1)} custom-call(s32[1]{0:T(128)} %bitcast.2.core, bf16[256,1024]{1,0:T(8,128)(2,1)} %get-tuple-element.37.refs_0_.refs_1_, bf16[256,1024]{1,0:T(8,128)(2,1)} %collective-permute-done.20.refs_0_.refs_2_.refs_1_, bf16[256,1024]{1,0:T(8,128)(2,1)} %collective-permute-done.21.refs_1_.refs_3_.refs_2_, ...), custom_call_target="tpu_custom_call" | custom-call | tf_op jit(solution)/shard_map/pallas_call | solution.py:322
  147.0 5.7 %shard_map.86 = (bf16[128,1536]{1,0:T(8,128)(2,1)}, bf16[128,1536]{1,0:T(8,128)(2,1)}) custom-call(s32[1]{0:T(128)} %bitcast.2.core, bf16[3,512,1536]{2,1,0:T(8,128)(2,1)} %own_weight.11, bf16[3,512,1536]{2,1,0:T(8,128)(2,1)} %collective-permute-done.other_weight, bf16[256,1024]{1,0:T(8,128)(2,1)} %get-tuple-element.37.refs_0_.refs_1_, ...), custom_call_target="tpu_custom_call" | custom-call | tf_op jit(solution)/shard_map/pallas_call | solution.py:184
  155.9 3.0 %shard_map.90 = (bf16[256,1536]{1,0:T(8,128)(2,1)}, bf16[256,1024]{1,0:T(8,128)(2,1)}) custom-call(f32[8,256]{1,0:T(8,128)} %get-tuple-element.28.places, bf16[256,1024]{1,0:T(8,128)(2,1)} %shard_map.83.term, bf16[128,1536]{1,0:T(8,128)(2,1)S(1)} %copy-done.4, bf16[128,1536]{1,0:T(8,128)(2,1)S(1)} %collective-permute-done.22.refs_1_, ...), custom_call_target="tpu_custom_call" | custom-call | tf_op jit(solution)/shard_map/pallas_call | solution.py:238
  (91 shorter events, 27.2 us)
Async XLA Ops:
  0.6 32.4 %collective-permute-start = (bf16[3,512,1536]{2,1,0:T(8,128)(2,1)}, bf16[3,512,1536]{2,1,0:T(8,128)(2,1)}, u32[]{:S(2)}, u32[]{:S(2)}) collective-permute-start(bf16[3,512,1536]{2,1,0:T(8,128)(2,1)} %own_weight.11), channel_id=1, source_target_pairs={{0,4},{4,0},{8,12},{12,8},{16,20},{20,16},{24,28},{28,24},{1,5},{5... | collective-permute-start | bytes 14155784 | tf_op jit(solution)/shard_map/ppermute | solution.py:364
  4.4 13.3 %collective-permute-start.3 = (bf16[136,1536]{1,0:T(8,128)(2,1)}, bf16[136,1536]{1,0:T(8,128)(2,1)}, u32[]{:S(2)}, u32[]{:S(2)}) collective-permute-start(bf16[136,1536]{1,0:T(8,128)(2,1)} %get-tuple-element.29.refs_0_.refs_2_.refs_8_.refs_24_), channel_id=1, source_target_pairs={{0,16},{4,20},{8,24},{12,28},{16,0},{20,4},{24,8},{28,12},{1,17},{... | collective-permute-start | bytes 1253384 | tf_op jit(solution)/shard_map/ppermute | solution.py:361
  9.1 15.9 %collective-permute-start.15 = (bf16[256,1024]{1,0:T(8,128)(2,1)}, bf16[256,1024]{1,0:T(8,128)(2,1)S(1)}, u32[]{:S(2)}, u32[]{:S(2)}) collective-permute-start(bf16[256,1024]{1,0:T(8,128)(2,1)} %shard_map.84.refs_0_), channel_id=1, source_target_pairs={{0,1},{1,0},{2,3},{3,2},{4,5},{5,4},{6,7},{7,6},{8,9},{9,8},{10,11... | collective-permute-start | bytes 1572872 | tf_op jit(solution)/shard_map/ppermute | solution.py:376
  10.7 12.8 %collective-permute-start.1 = (bf16[136,1536]{1,0:T(8,128)(2,1)}, bf16[136,1536]{1,0:T(8,128)(2,1)}, u32[]{:S(2)}, u32[]{:S(2)}) collective-permute-start(bf16[136,1536]{1,0:T(8,128)(2,1)} %get-tuple-element.29.refs_0_.refs_2_.refs_8_.refs_24_), channel_id=1, source_target_pairs={{0,8},{4,12},{8,0},{12,4},{16,24},{20,28},{24,16},{28,20},{1,9},{5... | collective-permute-start | bytes 1253384 | tf_op jit(solution)/shard_map/ppermute | solution.py:361
  12.2 14.3 %collective-permute-start.4 = (bf16[136,1536]{1,0:T(8,128)(2,1)}, bf16[136,1536]{1,0:T(8,128)(2,1)}, u32[]{:S(2)}, u32[]{:S(2)}) collective-permute-start(bf16[136,1536]{1,0:T(8,128)(2,1)} %get-tuple-element.30.refs_1_.refs_3_.refs_9_.refs_25_), channel_id=1, source_target_pairs={{0,16},{4,20},{8,24},{12,28},{16,0},{20,4},{24,8},{28,12},{1,17},{... | collective-permute-start | bytes 1253384 | tf_op jit(solution)/shard_map/ppermute | solution.py:361
  17.8 14.7 %collective-permute-start.2 = (bf16[136,1536]{1,0:T(8,128)(2,1)}, bf16[136,1536]{1,0:T(8,128)(2,1)}, u32[]{:S(2)}, u32[]{:S(2)}) collective-permute-start(bf16[136,1536]{1,0:T(8,128)(2,1)} %get-tuple-element.30.refs_1_.refs_3_.refs_9_.refs_25_), channel_id=1, source_target_pairs={{0,8},{4,12},{8,0},{12,4},{16,24},{20,28},{24,16},{28,20},{1,9},{5... | collective-permute-start | bytes 1253384 | tf_op jit(solution)/shard_map/ppermute | solution.py:361
  23.5 26.8 %collective-permute-start.16 = (bf16[256,1024]{1,0:T(8,128)(2,1)}, bf16[256,1024]{1,0:T(8,128)(2,1)}, u32[]{:S(2)}, u32[]{:S(2)}) collective-permute-start(bf16[256,1024]{1,0:T(8,128)(2,1)} %shard_map.84.refs_0_), channel_id=1, source_target_pairs={{1,2},{2,1},{5,6},{6,5},{9,10},{10,9},{13,14},{14,13},{17,18},{18,... | collective-permute-start | bytes 1572872 | tf_op jit(solution)/shard_map/ppermute | solution.py:376
  25.0 26.6 %collective-permute-start.18 = (bf16[256,1024]{1,0:T(8,128)(2,1)S(1)}, bf16[256,1024]{1,0:T(8,128)(2,1)}, u32[]{:S(2)}, u32[]{:S(2)}) collective-permute-start(bf16[256,1024]{1,0:T(8,128)(2,1)S(1)} %collective-permute-done.15.refs_1_), channel_id=1, source_target_pairs={{1,2},{2,1},{5,6},{6,5},{9,10},{10,9},{13,14},{14,13},{17,18},{18,... | collective-permute-start | bytes 1572872 | tf_op jit(solution)/shard_map/ppermute | solution.py:376
  26.5 15.6 %collective-permute-start.7 = (bf16[136,1536]{1,0:T(8,128)(2,1)}, bf16[136,1536]{1,0:T(8,128)(2,1)S(1)}, u32[]{:S(2)}, u32[]{:S(2)}) collective-permute-start(bf16[136,1536]{1,0:T(8,128)(2,1)} %collective-permute-done.3.refs_2_.refs_5_.refs_12_.refs_28_), channel_id=1, source_target_pairs={{0,8},{4,12},{8,0},{12,4},{16,24},{20,28},{24,16},{28,20},{1,9},{5... | collective-permute-start | bytes 1253384 | tf_op jit(solution)/shard_map/ppermute | solution.py:361
  40.6 14.4 %collective-permute-start.5 = (bf16[256,1024]{1,0:T(8,128)(2,1)}, bf16[256,1024]{1,0:T(8,128)(2,1)S(1)}, u32[]{:S(2)}, u32[]{:S(2)}) collective-permute-start(bf16[256,1024]{1,0:T(8,128)(2,1)} %get-tuple-element.31), channel_id=1, source_target_pairs={{0,8},{4,12},{8,0},{12,4},{16,24},{20,28},{24,16},{28,20},{1,9},{5... | collective-permute-start | bytes 1572872 | tf_op jit(solution)/shard_map/ppermute | solution.py:361
  42.1 22.8 %collective-permute-start.6 = (bf16[256,1024]{1,0:T(8,128)(2,1)}, bf16[256,1024]{1,0:T(8,128)(2,1)S(1)}, u32[]{:S(2)}, u32[]{:S(2)}) collective-permute-start(bf16[256,1024]{1,0:T(8,128)(2,1)} %get-tuple-element.32), channel_id=1, source_target_pairs={{0,16},{4,20},{8,24},{12,28},{16,0},{20,4},{24,8},{28,12},{1,17},{... | collective-permute-start | bytes 1572872 | tf_op jit(solution)/shard_map/ppermute | solution.py:361
  49.9 21.3 %collective-permute-start.9 = (bf16[256,1024]{1,0:T(8,128)(2,1)}, bf16[256,1024]{1,0:T(8,128)(2,1)S(1)}, u32[]{:S(2)}, u32[]{:S(2)}) collective-permute-start(bf16[256,1024]{1,0:T(8,128)(2,1)} %shard_map.79), channel_id=1, source_target_pairs={{0,24},{4,28},{8,16},{12,20},{16,8},{20,12},{24,0},{28,4},{1,25},{... | collective-permute-start | bytes 1572872 | tf_op jit(solution)/shard_map/ppermute | solution.py:361
  50.3 25.3 %collective-permute-start.17 = (bf16[256,1024]{1,0:T(8,128)(2,1)}, bf16[256,1024]{1,0:T(8,128)(2,1)}, u32[]{:S(2)}, u32[]{:S(2)}) collective-permute-start(bf16[256,1024]{1,0:T(8,128)(2,1)} %collective-permute-done.16.refs_2_), channel_id=1, source_target_pairs={{1,0},{2,3},{5,4},{6,7},{9,8},{10,11},{13,12},{14,15},{17,16},{18,... | collective-permute-start | bytes 1572872 | tf_op jit(solution)/shard_map/ppermute | solution.py:376
  51.6 24.3 %collective-permute-start.19 = (bf16[256,1024]{1,0:T(8,128)(2,1)}, bf16[256,1024]{1,0:T(8,128)(2,1)}, u32[]{:S(2)}, u32[]{:S(2)}) collective-permute-start(bf16[256,1024]{1,0:T(8,128)(2,1)} %collective-permute-done.18.refs_4_), channel_id=1, source_target_pairs={{1,0},{2,3},{5,4},{6,7},{9,8},{10,11},{13,12},{14,15},{17,16},{18,... | collective-permute-start | bytes 1572872 | tf_op jit(solution)/shard_map/ppermute | solution.py:376
  55.0 20.4 %collective-permute-start.33 = (bf16[136,1536]{1,0:T(8,128)(2,1)}, bf16[136,1536]{1,0:T(8,128)(2,1)}, u32[]{:S(2)}, u32[]{:S(2)}) collective-permute-start(bf16[136,1536]{1,0:T(8,128)(2,1)} %get-tuple-element.29.refs_0_.refs_2_.refs_8_.refs_24_), channel_id=1, source_target_pairs={{0,4},{4,0},{8,12},{12,8},{16,20},{20,16},{24,28},{28,24},{1,5},{5... | collective-permute-start | bytes 1253384 | tf_op jit(solution)/shard_map/ppermute | solution.py:364
  64.8 14.8 %collective-permute-start.34 = (bf16[136,1536]{1,0:T(8,128)(2,1)}, bf16[136,1536]{1,0:T(8,128)(2,1)}, u32[]{:S(2)}, u32[]{:S(2)}) collective-permute-start(bf16[136,1536]{1,0:T(8,128)(2,1)} %get-tuple-element.30.refs_1_.refs_3_.refs_9_.refs_25_), channel_id=1, source_target_pairs={{0,4},{4,0},{8,12},{12,8},{16,20},{20,16},{24,28},{28,24},{1,5},{5... | collective-permute-start | bytes 1253384 | tf_op jit(solution)/shard_map/ppermute | solution.py:364
  73.0 14.4 %collective-permute-start.10 = (bf16[256,1024]{1,0:T(8,128)(2,1)}, bf16[256,1024]{1,0:T(8,128)(2,1)S(1)}, u32[]{:S(2)}, u32[]{:S(2)}) collective-permute-start(bf16[256,1024]{1,0:T(8,128)(2,1)} %shard_map.80), channel_id=1, source_target_pairs={{0,1},{3,2},{4,5},{7,6},{8,9},{11,10},{12,13},{15,14},{16,17},{19,... | collective-permute-start | bytes 1572872 | tf_op jit(solution)/shard_map/ppermute | solution.py:376
  79.7 20.8 %collective-permute-start.23 = (bf16[256,1024]{1,0:T(8,128)(2,1)}, bf16[256,1024]{1,0:T(8,128)(2,1)}, u32[]{:S(2)}, u32[]{:S(2)}) collective-permute-start(bf16[256,1024]{1,0:T(8,128)(2,1)} %get-tuple-element.43), channel_id=1, source_target_pairs={{0,24},{4,28},{8,16},{12,20},{16,8},{20,12},{24,0},{28,4},{1,25},{... | collective-permute-start | bytes 1572872 | tf_op jit(solution)/shard_map/ppermute | solution.py:361
  87.5 19.0 %collective-permute-start.20 = (bf16[256,1024]{1,0:T(8,128)(2,1)}, bf16[256,1024]{1,0:T(8,128)(2,1)}, u32[]{:S(2)}, u32[]{:S(2)}) collective-permute-start(bf16[256,1024]{1,0:T(8,128)(2,1)} %get-tuple-element.39), channel_id=1, source_target_pairs={{0,8},{4,12},{8,0},{12,4},{16,24},{20,28},{24,16},{28,20},{1,9},{5... | collective-permute-start | bytes 1572872 | tf_op jit(solution)/shard_map/ppermute | solution.py:361
  90.7 17.0 %collective-permute-start.21 = (bf16[256,1024]{1,0:T(8,128)(2,1)}, bf16[256,1024]{1,0:T(8,128)(2,1)}, u32[]{:S(2)}, u32[]{:S(2)}) collective-permute-start(bf16[256,1024]{1,0:T(8,128)(2,1)} %get-tuple-element.40), channel_id=1, source_target_pairs={{0,16},{4,20},{8,24},{12,28},{16,0},{20,4},{24,8},{28,12},{1,17},{... | collective-permute-start | bytes 1572872 | tf_op jit(solution)/shard_map/ppermute | solution.py:361
  91.5 16.5 %collective-permute-start.11 = (bf16[256,1024]{1,0:T(8,128)(2,1)}, bf16[256,1024]{1,0:T(8,128)(2,1)S(1)}, u32[]{:S(2)}, u32[]{:S(2)}) collective-permute-start(bf16[256,1024]{1,0:T(8,128)(2,1)} %get-tuple-element.33), channel_id=1, source_target_pairs={{2,1},{1,2},{6,5},{5,6},{10,9},{9,10},{14,13},{13,14},{18,17},{17,... | collective-permute-start | bytes 1572872 | tf_op jit(solution)/shard_map/ppermute | solution.py:376
  92.2 18.8 %collective-permute-start.12 = (bf16[256,1024]{1,0:T(8,128)(2,1)}, bf16[256,1024]{1,0:T(8,128)(2,1)S(1)}, u32[]{:S(2)}, u32[]{:S(2)}) collective-permute-start(bf16[256,1024]{1,0:T(8,128)(2,1)} %get-tuple-element.34), channel_id=1, source_target_pairs={{0,1},{3,2},{4,5},{7,6},{8,9},{11,10},{12,13},{15,14},{16,17},{19,... | collective-permute-start | bytes 1572872 | tf_op jit(solution)/shard_map/ppermute | solution.py:376
  100.4 13.8 %collective-permute-start.29 = (bf16[256,1024]{1,0:T(8,128)(2,1)}, bf16[256,1024]{1,0:T(8,128)(2,1)}, u32[]{:S(2)}, u32[]{:S(2)}) collective-permute-start(bf16[256,1024]{1,0:T(8,128)(2,1)} %get-tuple-element.37.refs_0_.refs_1_), channel_id=1, source_target_pairs={{0,4},{4,0},{8,12},{12,8},{16,20},{20,16},{24,28},{28,24},{1,5},{5... | collective-permute-start | bytes 1572872 | tf_op jit(solution)/shard_map/ppermute | solution.py:364
  107.8 23.0 %collective-permute-start.30 = (bf16[256,1024]{1,0:T(8,128)(2,1)}, bf16[256,1024]{1,0:T(8,128)(2,1)S(1)}, u32[]{:S(2)}, u32[]{:S(2)}) collective-permute-start(bf16[256,1024]{1,0:T(8,128)(2,1)} %collective-permute-done.20.refs_0_.refs_2_.refs_1_), channel_id=1, source_target_pairs={{0,4},{4,0},{8,12},{12,8},{16,20},{20,16},{24,28},{28,24},{1,5},{5... | collective-permute-start | bytes 1572872 | tf_op jit(solution)/shard_map/ppermute | solution.py:364
  108.0 24.4 %collective-permute-start.31 = (bf16[256,1024]{1,0:T(8,128)(2,1)}, bf16[256,1024]{1,0:T(8,128)(2,1)S(1)}, u32[]{:S(2)}, u32[]{:S(2)}) collective-permute-start(bf16[256,1024]{1,0:T(8,128)(2,1)} %collective-permute-done.21.refs_1_.refs_3_.refs_2_), channel_id=1, source_target_pairs={{0,4},{4,0},{8,12},{12,8},{16,20},{20,16},{24,28},{28,24},{1,5},{5... | collective-permute-start | bytes 1572872 | tf_op jit(solution)/shard_map/ppermute | solution.py:364
  114.2 18.6 %collective-permute-start.32 = (bf16[256,1024]{1,0:T(8,128)(2,1)}, bf16[256,1024]{1,0:T(8,128)(2,1)S(1)}, u32[]{:S(2)}, u32[]{:S(2)}) collective-permute-start(bf16[256,1024]{1,0:T(8,128)(2,1)} %collective-permute-done.23.refs_0_.refs_1_.refs_3_), channel_id=1, source_target_pairs={{0,4},{4,0},{8,12},{12,8},{16,20},{20,16},{24,28},{28,24},{1,5},{5... | collective-permute-start | bytes 1572872 | tf_op jit(solution)/shard_map/ppermute | solution.py:364
  118.1 16.2 %collective-permute-start.13 = (bf16[256,1024]{1,0:T(8,128)(2,1)}, bf16[256,1024]{1,0:T(8,128)(2,1)S(1)}, u32[]{:S(2)}, u32[]{:S(2)}) collective-permute-start(bf16[256,1024]{1,0:T(8,128)(2,1)} %get-tuple-element.35), channel_id=1, source_target_pairs={{1,0},{0,1},{3,2},{2,3},{5,4},{4,5},{7,6},{6,7},{9,8},{8,9},{11,10... | collective-permute-start | bytes 1572872 | tf_op jit(solution)/shard_map/ppermute | solution.py:376
  120.2 32.5 %collective-permute-start.14 = (bf16[256,1024]{1,0:T(8,128)(2,1)}, bf16[256,1024]{1,0:T(8,128)(2,1)S(1)}, u32[]{:S(2)}, u32[]{:S(2)}) collective-permute-start(bf16[256,1024]{1,0:T(8,128)(2,1)} %get-tuple-element.36), channel_id=1, source_target_pairs={{2,1},{1,2},{6,5},{5,6},{10,9},{9,10},{14,13},{13,14},{18,17},{17,... | collective-permute-start | bytes 1572872 | tf_op jit(solution)/shard_map/ppermute | solution.py:376
  130.8 23.0 %collective-permute-start.22 = (bf16[128,1536]{1,0:T(8,128)(2,1)}, bf16[128,1536]{1,0:T(8,128)(2,1)S(1)}, u32[]{:S(2)}, u32[]{:S(2)}) collective-permute-start(bf16[128,1536]{1,0:T(8,128)(2,1)} %get-tuple-element.41), channel_id=1, source_target_pairs={{0,8},{4,12},{8,0},{12,4},{16,24},{20,28},{24,16},{28,20},{1,9},{5... | collective-permute-start | bytes 1179656 | tf_op jit(solution)/shard_map/ppermute | solution.py:361
  132.3 21.5 %collective-permute-start.28 = (bf16[128,1536]{1,0:T(8,128)(2,1)}, bf16[128,1536]{1,0:T(8,128)(2,1)}, u32[]{:S(2)}, u32[]{:S(2)}) collective-permute-start(bf16[128,1536]{1,0:T(8,128)(2,1)} %get-tuple-element.50), channel_id=1, source_target_pairs={{0,16},{4,20},{8,24},{12,28},{16,0},{20,4},{24,8},{28,12},{1,17},{... | collective-permute-start | bytes 1179656 | tf_op jit(solution)/shard_map/ppermute | solution.py:361
  132.8 21.0 %collective-permute-start.26 = (bf16[128,1536]{1,0:T(8,128)(2,1)}, bf16[128,1536]{1,0:T(8,128)(2,1)}, u32[]{:S(2)}, u32[]{:S(2)}) collective-permute-start(bf16[128,1536]{1,0:T(8,128)(2,1)} %get-tuple-element.47), channel_id=1, source_target_pairs={{0,16},{4,20},{8,24},{12,28},{16,0},{20,4},{24,8},{28,12},{1,17},{... | collective-permute-start | bytes 1179656 | tf_op jit(solution)/shard_map/ppermute | solution.py:361
  134.4 19.5 %collective-permute-start.27 = (bf16[128,1536]{1,0:T(8,128)(2,1)}, bf16[128,1536]{1,0:T(8,128)(2,1)}, u32[]{:S(2)}, u32[]{:S(2)}) collective-permute-start(bf16[128,1536]{1,0:T(8,128)(2,1)} %get-tuple-element.49), channel_id=1, source_target_pairs={{0,8},{4,12},{8,0},{12,4},{16,24},{20,28},{24,16},{28,20},{1,9},{5... | collective-permute-start | bytes 1179656 | tf_op jit(solution)/shard_map/ppermute | solution.py:361
  (20 other events, 207.8 us)
